TPU v7x, 32 devices: a whole 2x2x4 slice. The times are simulated.
32 devices in a mesh: dp: 8 (over z, x), row: 2 (over core), col: 2 (over y).
Axes of the slice: x: 2, y: 2, z: 4, core: 2. Of those that a mesh axis runs over, the one named last changes fastest.
Arguments:
- tokens: bfloat16 [2, 8, 256, 2048], P(None, None, 'dp', ('row', 'col')), may hold values from -57 to 57
- lengths: int32 [2, 8], replicated, may hold values from 64 to 256, as said below
- deal_order: int32 [2, 8], replicated, may hold values from 0 to 7, each once within a row
- attention_gain: float32 [2048], P(('row', 'col')), may hold values from 0.25 to 1.75
- query_weight: bfloat16 [2048, 2048], P('row', 'col'), may hold values from -0.1875 to 0.1875
- key_weight: bfloat16 [2048, 2048], P('row', 'col'), may hold values from -0.1875 to 0.1875
- value_weight: bfloat16 [2048, 2048], P('row', 'col'), may hold values from -0.125 to 0.125
- output_weight: bfloat16 [2048, 2048], P('col', 'row'), may hold values from -0.25 to 0.25
- feed_gain: float32 [2048], P(('row', 'col')), may hold values from 0.25 to 1.75
- gate_weight: bfloat16 [2048, 8192], P('row', 'col'), may hold values from -0.125 to 0.125
- up_weight: bfloat16 [2048, 8192], P('row', 'col'), may hold values from -0.125 to 0.125
- down_weight: bfloat16 [8192, 2048], P('col', 'row'), may hold values from -0.09375 to 0.09375
- cotangent: bfloat16 [2, 8, 256, 2048], P(None, 'dp', None, ('row', 'col')), may hold values from -6 to 6
Outputs:
- layer_output: bfloat16 [2, 8, 256, 2048], P(None, None, 'dp', ('row', 'col'))
- tokens_grad: bfloat16 [2, 8, 256, 2048], P(None, None, 'dp', ('row', 'col'))
- attention_gain_grad: float32 [2048], P(('row', 'col', 'dp'))
- query_grad: float32 [2048, 2048], P(('row', 'dp'), 'col')
- key_grad: float32 [2048, 2048], P(('row', 'dp'), 'col')
- value_grad: float32 [2048, 2048], P(('row', 'dp'), 'col')
- output_grad: float32 [2048, 2048], P(('col', 'dp'), 'row')
- feed_gain_grad: float32 [2048], P(('row', 'col', 'dp'))
- gate_grad: float32 [2048, 8192], P(('row', 'dp'), 'col')
- up_grad: float32 [2048, 8192], P(('row', 'dp'), 'col')
- down_grad: float32 [8192, 2048], P(('col', 'dp'), 'row')
Inputs may be any that keep to these rules, and one draw needn't show every extreme that they name: `lengths`: in each micro-batch one sequence has exactly 256 tokens. `deal_order`: each row holds every number of 0 to 7 once.
All inputs are finite; a program needn't handle non-finite values.
Results may differ from a plain program's by a relative error of at most 0.023.
Values may be sent and summed in bfloat16 or wider, within the bound.
A program may use at most 256 MiB of HBM per device.

v0:
```python
import math

import jax
import jax.numpy as jnp
from jax import lax
from jax.experimental import pallas as pl
from jax.experimental.pallas import tpu as pltpu
from jax.sharding import PartitionSpec as P

D = 2048
HEADS = 32
HEAD_DIM = 64
SL = 256
MICRO = 2
ROWS = MICRO * SL

EPSILON = 1e-05
ROPE_THETA = 130000.0
MASKED_SCORE = -1000000000.0
F32 = jnp.float32
BF16 = jnp.bfloat16
SWAP = [(0, 1), (1, 0)]


def mm(a, b):
    return jnp.dot(a, b, preferred_element_type=F32)


def mm_nt(a, b):
    return lax.dot_general(a, b, (((1,), (1,)), ((), ())), preferred_element_type=F32)


def mm_tn(a, b):
    return lax.dot_general(a, b, (((0,), (0,)), ((), ())), preferred_element_type=F32)


def rope_tables():
    half = HEAD_DIM // 2
    frequency = jnp.exp(
        jnp.arange(half, dtype=F32) * (-2.0 * math.log(ROPE_THETA) / HEAD_DIM)
    )
    angles = jnp.arange(SL, dtype=F32)[:, None] * frequency[None, :]
    cosine = jnp.cos(angles)
    sine = jnp.sin(angles)
    zero = jnp.zeros_like(sine)
    table_cos = jnp.concatenate([cosine] * 4, axis=1)
    table_first = jnp.concatenate([sine, zero] * 2, axis=1)
    table_second = jnp.concatenate([zero, sine] * 2, axis=1)
    return table_cos, table_first, table_second


def turn(v, cos, first, second):
    ahead = pltpu.roll(v, 128 - HEAD_DIM // 2, 1)
    behind = pltpu.roll(v, HEAD_DIM // 2, 1)
    return v * cos - ahead * first + behind * second


def turn_back(v, cos, first, second):
    ahead = pltpu.roll(v, 128 - HEAD_DIM // 2, 1)
    behind = pltpu.roll(v, HEAD_DIM // 2, 1)
    return v * cos + ahead * first - behind * second


def head_mask(head):
    lane = lax.broadcasted_iota(jnp.int32, (SL, 128), 1)
    return (lane // HEAD_DIM) == head


def softmax_of(q, k, allowed):
    scores = mm_nt(q, k) * HEAD_DIM ** (-0.5)
    scores = jnp.where(allowed, scores, MASKED_SCORE)
    exps = jnp.exp(scores - jnp.max(scores, axis=1, keepdims=True))
    return exps / jnp.sum(exps, axis=1, keepdims=True)


def allowed_of(length):
    query = lax.broadcasted_iota(jnp.int32, (SL, SL), 0)
    key = lax.broadcasted_iota(jnp.int32, (SL, SL), 1)
    return (key <= query) & (key < length)


FREE = pl.CostEstimate(flops=0, bytes_accessed=0, transcendentals=0)
BUSY = pl.CostEstimate(flops=20 * 10**9, bytes_accessed=60 * 10**6, transcendentals=0)


def whole(shape):
    return pl.BlockSpec(shape, lambda *at: (0,) * len(shape), pipeline_mode=pl.Buffered(1))


def attend_kernel(len_ref, qkv_ref, cos_ref, first_ref, second_ref, o_ref, turned_ref):
    cos, first, second = cos_ref[...], first_ref[...], second_ref[...]
    qr = turn(qkv_ref[:, :128], cos, first, second).astype(BF16)
    kr = turn(qkv_ref[:, 128:256], cos, first, second).astype(BF16)
    vr = qkv_ref[:, 256:].astype(BF16)
    turned_ref[:, :128] = qr
    turned_ref[:, 128:256] = kr
    turned_ref[:, 256:] = vr
    allowed = allowed_of(len_ref[pl.program_id(0)])
    out = jnp.zeros((SL, 128), F32)
    for head in range(2):
        mask = head_mask(head)
        probs = softmax_of(jnp.where(mask, qr, jnp.zeros_like(qr)), kr, allowed).astype(BF16)
        out = out + mm(probs, jnp.where(mask, vr, jnp.zeros_like(vr)))
    o_ref[...] = out.astype(BF16)


def head_grads(qr, kr, vr, od, allowed, cos, first, second):
    dq = jnp.zeros((SL, 128), F32)
    dk = jnp.zeros((SL, 128), F32)
    dv = jnp.zeros((SL, 128), F32)
    zero = jnp.zeros_like(qr)
    for head in range(2):
        mask = head_mask(head)
        q_own = jnp.where(mask, qr, zero)
        k_own = jnp.where(mask, kr, zero)
        od_own = jnp.where(mask, od, zero)
        probs = softmax_of(q_own, kr, allowed)
        d_probs = mm_nt(od_own, vr)
        dv = dv + mm_tn(probs.astype(BF16), od_own)
        inner = jnp.sum(probs * d_probs, axis=1, keepdims=True)
        d_scores = (probs * (d_probs - inner)).astype(BF16)
        dq = dq + mm(d_scores, k_own)
        dk = dk + mm_tn(d_scores, q_own)
    scale = HEAD_DIM ** (-0.5)
    return (
        turn_back(dq * scale, cos, first, second).astype(BF16),
        turn_back(dk * scale, cos, first, second).astype(BF16),
        dv.astype(BF16),
    )


def pair_block(width):
    return pl.BlockSpec((SL, width), lambda m, h, lens: (m, h))


TABLE = pl.BlockSpec((SL, 128), lambda m, h, lens: (0, 0))


def attend_forward(lengths, qkv, tables):
    width = qkv.shape[1]
    return pl.pallas_call(
        attend_kernel,
        out_shape=(
            jax.ShapeDtypeStruct((ROWS, width // 3), BF16),
            jax.ShapeDtypeStruct((ROWS, width), BF16),
        ),
        grid_spec=pltpu.PrefetchScalarGridSpec(
            num_scalar_prefetch=1,
            grid=(MICRO, width // 384),
            in_specs=[pair_block(384)] + [TABLE] * 3,
            out_specs=[pair_block(128), pair_block(384)],
        ),
        cost_estimate=FREE,
    )(lengths, qkv, *tables)


def multiply(a, w, transposed, tile, dtype):
    height, depth = a.shape
    width = w.shape[0] if transposed else w.shape[1]

    def kernel(a_ref, w_ref, o_ref):
        form = mm_nt if transposed else mm
        o_ref[...] = form(a_ref[...], w_ref[...]).astype(dtype)

    if transposed:
        w_spec = pl.BlockSpec((tile, depth), lambda j: (j, 0))
    else:
        w_spec = pl.BlockSpec((depth, tile), lambda j: (0, j))
    return pl.pallas_call(
        kernel,
        out_shape=jax.ShapeDtypeStruct((height, width), dtype),
        grid=(width // tile,),
        in_specs=[whole(a.shape), w_spec],
        out_specs=pl.BlockSpec((height, tile), lambda j: (0, j)),
        cost_estimate=FREE,
    )(a, w)


def split_product(parts, w, transposed, tile, cost=FREE):
    count = len(parts)
    height = parts[0].shape[0]
    width = w.shape[0] if transposed else w.shape[1]
    steps = width // tile
    half = steps // 2

    def kernel(*refs):
        form = mm_nt if transposed else mm
        total = form(refs[0][...], refs[count][...])
        for at in range(1, count):
            total = total + form(refs[at][...], refs[count + at][...])
        kept_ref, sent_ref = refs[2 * count :]
        step = pl.program_id(0)

        @pl.when(step < half)
        def _():
            sent_ref[...] = total.astype(BF16)

        @pl.when(step >= half)
        def _():
            kept_ref[...] = total

    def w_spec(at, depth):
        if transposed:
            return pl.BlockSpec((tile, depth), lambda j: (lax.rem(j + half, steps), at))
        return pl.BlockSpec((depth, tile), lambda j: (at, lax.rem(j + half, steps)))

    return pl.pallas_call(
        kernel,
        out_shape=(
            jax.ShapeDtypeStruct((height, width // 2), F32),
            jax.ShapeDtypeStruct((height, width // 2), BF16),
        ),
        grid=(steps,),
        in_specs=[whole(part.shape) for part in parts]
        + [w_spec(at, part.shape[1]) for at, part in enumerate(parts)],
        out_specs=(
            pl.BlockSpec((height, tile), lambda j: (0, jnp.maximum(j - half, 0))),
            pl.BlockSpec((height, tile), lambda j: (0, jnp.minimum(j, half - 1))),
        ),
        cost_estimate=cost,
    )(*parts, *([w] * count))


def feed_kernel(x_ref, gate_ref, up_ref, da_ref, hidden_ref, dg_ref, du_ref):
    x = x_ref[...]
    gate = mm(x, gate_ref[...])
    up = mm(x, up_ref[...])
    da = da_ref[...]
    sigmoid = 1.0 / (1.0 + jnp.exp(-gate))
    swish = gate * sigmoid
    hidden_ref[...] = (swish * up).astype(BF16)
    dg_ref[...] = (da * up * sigmoid * (1.0 + gate * (1.0 - sigmoid))).astype(BF16)
    du_ref[...] = (da * swish).astype(BF16)


def feed_forward(x, pair_w, hidden_grad, tile=256):
    height, depth = x.shape
    width = hidden_grad.shape[1]
    steps = width // tile
    tall = pl.BlockSpec((height, tile), lambda j: (0, j))
    return pl.pallas_call(
        feed_kernel,
        out_shape=(jax.ShapeDtypeStruct((height, width), BF16),) * 3,
        grid=(steps,),
        in_specs=[
            whole(x.shape),
            pl.BlockSpec((depth, tile), lambda j: (0, j)),
            pl.BlockSpec((depth, tile), lambda j: (0, j + steps)),
            tall,
        ],
        out_specs=(tall,) * 3,
        cost_estimate=FREE,
    )(x, pair_w, pair_w, hidden_grad)


def swap_kernel(plan, given, count, *refs):
    weights, outs = refs[:given], refs[given : given + count]
    rest = refs[given + count :]
    held, (send_sem, recv_sem, in_sem, out_sem) = rest[: len(plan)], rest[len(plan) :]
    row = lax.axis_index("row")
    barrier = pltpu.get_barrier_semaphore()
    pl.semaphore_signal(
        barrier, inc=1, device_id={"row": 1 - row}, device_id_type=pl.DeviceIdType.MESH
    )
    remote, local = [], []
    for at, (source, by_rows, out, start, offset, size) in enumerate(plan):
        weight = weights[source]
        height, width = weight.shape

        def part(index):
            if by_rows:
                return weight.at[pl.ds(pl.multiple_of(index * size, size), size), :]
            first = pl.multiple_of(index * (width // 2) + start, 128)
            return weight.at[:, pl.ds(first, size)]

        def place(second):
            if by_rows:
                return outs[out].at[:, pl.ds(second * width, width)]
            return outs[out].at[pl.ds(second * height, height), pl.ds(offset, size)]

        remote.append(
            pltpu.make_async_remote_copy(
                src_ref=part(1 - row),
                dst_ref=place(1),
                send_sem=send_sem.at[at],
                recv_sem=recv_sem.at[at],
                device_id={"row": 1 - row},
                device_id_type=pl.DeviceIdType.MESH,
            )
        )
        local.append(
            (
                pltpu.make_async_copy(part(row), held[at], in_sem.at[at]),
                pltpu.make_async_copy(held[at], place(0), out_sem.at[at]),
            )
        )
    for fetch, _ in local:
        fetch.start()
    pl.semaphore_wait(barrier, 1)
    for copy in remote:
        copy.start()
    for fetch, store in local:
        fetch.wait()
        store.start()
    for _, store in local:
        store.wait()
    for copy in remote:
        copy.wait()


def swap_weights(weights, plan, shapes, identity):
    held = []
    for source, by_rows, _, _, _, size in plan:
        height, width = weights[source].shape
        held.append((size, width) if by_rows else (height, size))
    sems = pltpu.SemaphoreType.DMA((len(plan),))
    return pl.pallas_call(
        lambda *refs: swap_kernel(plan, len(weights), len(shapes), *refs),
        out_shape=[jax.ShapeDtypeStruct(shape, BF16) for shape in shapes],
        in_specs=[pl.BlockSpec(memory_space=pl.ANY)] * len(weights),
        out_specs=[pl.BlockSpec(memory_space=pl.ANY)] * len(shapes),
        scratch_shapes=[pltpu.VMEM(shape, BF16) for shape in held] + [sems] * 4,
        compiler_params=pltpu.CompilerParams(collective_id=identity, has_side_effects=True),
        cost_estimate=FREE,
    )(*weights)


MESH = pl.DeviceIdType.MESH


def greet(*moves):
    barrier = pltpu.get_barrier_semaphore()
    total = 0
    for count, target in moves:
        total = total + count

        @pl.when(count > 0)
        def _():
            pl.semaphore_signal(barrier, inc=1, device_id=target, device_id_type=MESH)

    pl.semaphore_wait(barrier, total)


class ZLine:
    def __init__(self, line, grads, out, stage, came, sems, count, sided):
        self.line, self.grads, self.out, self.stage = line, grads, out, stage
        self.came, self.sems, self.sided = came, sems, sided
        width = grads.shape[1] // count
        self.pieces = [(k, pl.ds(k * width, width)) for k in range(count)]
        self.dp, self.row = lax.axis_index("dp"), lax.axis_index("row")
        self.z = self.dp // 2
        self.last = line - 1
        self.ways = ((0, self.z, 2), (1, self.last - self.z, -2))

    def rows_of(self, dest):
        size = self.grads.shape[0] // self.line
        if self.sided:
            dest = lax.rem(dest + self.line - self.row * (self.line // 2), self.line)
        return pl.ds(pl.multiple_of(dest * size, size), size)

    def copy(self, source, way, step, slot, piece, columns):
        return pltpu.make_async_remote_copy(
            src_ref=source,
            dst_ref=self.came.at[way, slot, :, columns],
            send_sem=self.sems.at[0, way, slot, piece],
            recv_sem=self.sems.at[1, way, slot, piece],
            device_id={"dp": self.dp + step},
            device_id_type=MESH,
        )

    def arrived(self, way, step, slot, piece, columns):
        held = self.came.at[way, slot, :, columns]
        self.copy(held, way, step, slot, piece, columns).wait_recv()
        return held

    def run(self, start, stop):
        def one_step(slot, _):
            for piece, columns in self.pieces:
                for way, place, step in self.ways:
                    far = self.last - slot + place
                    dest = far if step > 0 else self.last - far

                    @pl.when((place == 0) & (place < self.last))
                    def _():
                        source = self.grads.at[self.rows_of(dest), columns]
                        self.copy(source, way, step, slot, piece, columns).start()

                    @pl.when((place > 0) & (place <= slot))
                    def _():
                        held = self.arrived(way, step, slot - 1, piece, columns)

                        @pl.when(place < self.last)
                        def _():
                            held[...] = (
                                held[...].astype(F32)
                                + self.grads[self.rows_of(dest), columns].astype(F32)
                            ).astype(BF16)
                            self.copy(held, way, step, slot, piece, columns).start()

            return 0

        lax.fori_loop(start, stop, one_step, 0)

    def finish(self):
        own = self.rows_of(self.z)
        for piece, columns in self.pieces:
            self.stage[:, columns] = self.grads[own, columns].astype(F32)
            for way, place, step in self.ways:

                @pl.when(place > 0)
                def _():
                    held = self.arrived(way, step, self.last - 1, piece, columns)
                    self.stage[:, columns] += held[...].astype(F32)

        def settle(slot, _):
            for piece, columns in self.pieces:
                for way, place, step in self.ways:

                    @pl.when((place <= slot) & (place < self.last))
                    def _():
                        held = self.came.at[way, slot, :, columns]
                        self.copy(held, way, step, slot, piece, columns).wait_send()

            return 0

        lax.fori_loop(0, self.last, settle, 0)

    def moves(self):
        return (
            (jnp.minimum(self.z, 1), {"dp": self.dp - 2}),
            (jnp.minimum(self.last - self.z, 1), {"dp": self.dp + 2}),
        )


def tiles_loop(width, tile, body):
    def one(j, _):
        body(pl.ds(pl.multiple_of(j * tile, tile), tile), j * tile)
        return 0

    lax.fori_loop(0, width // tile, one, 0)


def tail_kernel(
    line,
    gate_grads,
    up,
    up_row,
    second_mine,
    second_came,
    dqkv,
    dqkv_row,
    first_mine,
    first_came,
    branch,
    mixed_mine,
    mixed_came,
    mixed_row,
    mixed_came_row,
    both,
    pieces,
    gate_out,
    up_out,
    query_out,
    key_out,
    value_out,
    output_out,
    back,
    gains_out,
    gate_z,
    up_z,
    qkv_z,
    output_z,
    up_grads,
    qkv_grads,
    output_grads,
    up_came,
    up_came_row,
    dqkv_came,
    dqkv_came_row,
    branch_came,
    turned_left,
    gate_stage,
    up_stage,
    qkv_stage,
    output_stage,
    gate_sems,
    up_sems,
    qkv_sems,
    output_sems,
    swap_sems,
    out_sems,
    gains,
    back_sems,
    gain_sems,
):
    groups = 2 * line
    dp, row = lax.axis_index("dp"), lax.axis_index("row")
    partner = dp + 1 - 2 * lax.rem(dp, 2)
    gate_line = ZLine(line, gate_grads, gate_out, gate_stage, gate_z, gate_sems, 4, False)
    up_line = ZLine(line, up_grads, up_out, up_stage, up_z, up_sems, 4, False)
    qkv_line = ZLine(line, qkv_grads, None, qkv_stage, qkv_z, qkv_sems, 3, False)
    output_line = ZLine(line, output_grads, output_out, output_stage, output_z, output_sems, 1, True)

    def swap(source, target, at, device):
        return pltpu.make_async_remote_copy(
            src_ref=source,
            dst_ref=target,
            send_sem=swap_sems.at[0, at],
            recv_sem=swap_sems.at[1, at],
            device_id=device,
            device_id_type=MESH,
        )

    up_x = swap(up, up_came, 0, {"dp": partner})
    branch_x = swap(branch, branch_came, 1, {"dp": partner})
    dqkv_x = swap(dqkv, dqkv_came, 2, {"dp": partner})
    up_across = swap(up_came, up_came_row, 3, {"row": 1 - row})
    dqkv_across = swap(dqkv_came, dqkv_came_row, 4, {"row": 1 - row})

    stores = []

    def store(source, target):
        copy = pltpu.make_async_copy(source, target, out_sems.at[len(stores)])
        copy.start()
        stores.append(copy)

    def store_wide(line_of):
        size = line_of.stage.shape[1] // 2
        for part in range(2):
            place = row if part == 0 else 1 - row
            there = pl.ds(pl.multiple_of(place * size, size), size)
            store(line_of.stage.at[:, pl.ds(part * size, size)], line_of.out.at[:, there])

    def store_qkv():
        heads = dqkv.shape[1] // 3
        for part in range(2):
            place = row if part == 0 else 1 - row
            for pair in range(heads // 128):
                for kind, out in enumerate((query_out, key_out, value_out)):
                    here = pl.ds(part * 3 * heads + pair * 384 + kind * 128, 128)
                    there = pl.ds(pl.multiple_of(place * heads + pair * 128, 128), 128)
                    store(qkv_stage.at[:, here], out.at[:, there])

    def returned(step):
        target = lax.rem(dp + step, groups)
        return pltpu.make_async_remote_copy(
            src_ref=both.at[:, target],
            dst_ref=back.at[:, dp],
            send_sem=back_sems.at[0, step],
            recv_sem=back_sems.at[1, step],
            device_id={"dp": target},
            device_id_type=MESH,
        )

    gain_steps = groups.bit_length() - 1

    def gain_copy(step):
        reach = 1 << step
        peer = dp + reach - 2 * reach * lax.rem(dp // reach, 2)
        return pltpu.make_async_remote_copy(
            src_ref=gains.at[0, step],
            dst_ref=gains.at[1, step],
            send_sem=gain_sems.at[0, step],
            recv_sem=gain_sems.at[1, step],
            device_id={"dp": peer},
            device_id_type=MESH,
        )

    def gain_step(step):
        if step >= gain_steps:
            return
        gain_copy(step).wait_recv()
        total = gains[0, step] + gains[1, step]
        if step + 1 == gain_steps:
            gains_out[...] = total
        else:
            gains[0, step + 1] = total
            gain_copy(step + 1).start()

    others = [(jnp.int32(1), {"dp": lax.rem(dp + step, groups)}) for step in range(1, groups)]
    greet(*others, (jnp.int32(1), {"row": 1 - row}))
    gains[0, 0] = pieces[...]
    gain_copy(0).start()
    gate_line.run(0, 1)
    up_x.start()
    branch_x.start()
    dqkv_x.start()

    def send_back(step, _):
        returned(step).start()
        return 0

    lax.fori_loop(1, groups, send_back, 0)
    store(both.at[:, dp], back.at[:, dp])

    depth = second_mine.shape[0]
    turned_left[:, :depth] = second_mine[...].T
    turned_left[:, depth:] = second_came[...].T
    gate_line.run(1, 2)

    def wide(target, shift, mine, came):
        def body(columns, start):
            total = mm(turned_left[:, :depth], mine[:, columns])
            total = total + mm(turned_left[:, depth:], came[:, columns])
            tile = total.shape[1]
            target[:, pl.ds(pl.multiple_of(shift + start, tile), tile)] = total.astype(BF16)

        tiles_loop(mine.shape[1], 512, body)

    up_x.wait_recv()
    up_across.start()
    gain_step(0)
    gate_line.run(2, line - 1)
    wide(up_grads, 0, up, up_came)
    up_across.wait_recv()
    wide(up_grads, up.shape[1], up_row, up_came_row)
    up_line.run(0, 1)
    gate_line.finish()
    store_wide(gate_line)

    turned_left[:, :depth] = first_mine[...].T
    turned_left[:, depth:] = first_came[...].T
    branch_x.wait_recv()

    def side(start, mine, came):
        def body(columns, _):
            total = mm_tn(mine[...], branch[:, columns]) + mm_tn(came[...], branch_came[:, columns])
            output_grads[pl.ds(start, mine.shape[1]), columns] = total.astype(BF16)

        tiles_loop(branch.shape[1], 512, body)

    side(0, mixed_mine, mixed_came)
    side(mixed_mine.shape[1], mixed_row, mixed_came_row)
    output_line.run(0, 1)
    up_line.run(1, 2)
    gain_step(1)
    dqkv_x.wait_recv()
    dqkv_across.start()
    wide(qkv_grads, 0, dqkv, dqkv_came)
    dqkv_across.wait_recv()
    wide(qkv_grads, dqkv.shape[1], dqkv_row, dqkv_came_row)
    qkv_line.run(0, 1)
    output_line.run(1, 2)
    up_line.run(2, line - 1)
    qkv_line.run(1, 2)
    output_line.run(2, line - 1)
    for step in range(2, gain_steps):
        gain_step(step)
    up_line.finish()
    store_wide(up_line)
    qkv_line.run(2, line - 1)
    output_line.finish()
    store(output_stage, output_out)
    qkv_line.finish()
    store_qkv()

    def get_back(step, _):
        returned(step).wait()
        return 0

    lax.fori_loop(1, groups, get_back, 0)
    for step in range(gain_steps):
        gain_copy(step).wait_send()
    for copy in (up_x, branch_x, dqkv_x, up_across, dqkv_across):
        copy.wait_send()
    for copy in stores:
        copy.wait()


def stream(source_of, slots_of, sems, count, body):
    def fetch(j, slot):
        return [
            pltpu.make_async_copy(source, target, sems.at[slot, k])
            for k, (source, target) in enumerate(zip(source_of(j), slots_of(slot)))
        ]

    for copy in fetch(0, 0):
        copy.start()

    def one(j, _):
        slot = lax.rem(j, 2)

        @pl.when(j + 1 < count)
        def _():
            for copy in fetch(j + 1, 1 - slot):
                copy.start()

        for copy in fetch(j, slot):
            copy.wait()
        body(j, slot)
        return 0

    lax.fori_loop(0, count, one, 0)


def rows_loop(body, size=64):
    def one(j, _):
        body(pl.ds(pl.multiple_of(j * size, size), size))
        return 0

    lax.fori_loop(0, ROWS // size, one, 0)


def chain_kernel(
    line,
    hidden,
    gate_grad,
    up_grad,
    second_mine,
    second_theirs,
    top_half,
    top_came,
    mixed_came,
    pair_w,
    down_w,
    qkv_w,
    out_w,
    turned,
    middle,
    inverse_first,
    inverse_second,
    gain_second,
    gain_first,
    x_own,
    key_live,
    cos,
    first,
    second,
    down_out,
    gate_grads,
    second_came,
    up_row,
    dqkv,
    dqkv_row,
    branch,
    mixed_came_row,
    both_out,
    pieces_out,
    gate_row,
    gate_came,
    gate_came_row,
    tiles,
    tall_tiles,
    pair_tiles,
    kept,
    sent,
    row_came,
    summed,
    col_came,
    block_sent,
    block_came,
    hidden_row,
    hidden_came,
    hidden_came_row,
    branch_row,
    dots,
    down_grads,
    down_z,
    middle_own,
    layer_own,
    first_own,
    mixed_grad,
    turned_left,
    feed_sum,
    attention_sum,
    swap_sems,
    piece_sems,
    tile_sems,
    down_sems,
    copy_sems,
):
    dp, row, col = lax.axis_index("dp"), lax.axis_index("row"), lax.axis_index("col")
    x = lax.rem(dp, 2)
    partner = {"dp": dp + 1 - 2 * x}
    across = {"row": 1 - row}
    beside = {"col": 1 - col}
    down_line = ZLine(line, down_grads, down_out, None, down_z, down_sems, 4, True)
    half = D // 2
    block = D // 4
    quarter = hidden.shape[1]
    pending = []

    def swap(source, target, at, device, sems=swap_sems):
        copy = pltpu.make_async_remote_copy(
            src_ref=source,
            dst_ref=target,
            send_sem=sems.at[0, at],
            recv_sem=sems.at[1, at],
            device_id=device,
            device_id_type=MESH,
        )
        return copy

    def begin(copy):
        copy.start()
        pending.append(copy)
        return copy

    greet(
        *down_line.moves(),
        (jnp.int32(1), partner),
        (jnp.int32(1), across),
        (jnp.int32(1), beside),
    )

    per = line // 2
    width = quarter // line

    def hidden_part(index, at):
        return hidden.at[:, pl.ds(pl.multiple_of((2 * at + index) * width, width), width)]

    to_x, to_row, on_row = [], [], []
    for at in range(per):
        there = pl.ds(at * width, width)
        to_x.append(
            begin(swap(hidden_part(1 - x, at), hidden_came.at[:, there], at, partner, piece_sems))
        )
    for at in range(per):
        there = pl.ds(at * width, width)
        to_row.append(
            begin(swap(hidden_part(x, at), hidden_row.at[:, there], per + at, across, piece_sems))
        )
    second_x = begin(swap(second_theirs, second_came, 0, partner))
    gate_x = begin(swap(gate_grad, gate_came, 1, partner))

    def nt_product(w, depth, start, body):
        stream(
            lambda j: [w.at[pl.ds(pl.multiple_of(start + j * 256, 256), 256), :]],
            lambda slot: [tiles.at[slot, :, pl.ds(0, depth)]],
            tile_sems,
            half // 256,
            body,
        )

    def columns_at(j, size=256):
        return pl.ds(pl.multiple_of(j * size, size), size)

    def pair_body(target, dtype):
        def body(j, slot):
            total = mm_nt(gate_grad[...], tiles[slot, :, :quarter])
            total = total + mm_nt(up_grad[...], tiles[slot, :, quarter:])
            target[:, columns_at(j)] = total.astype(dtype)

        return body

    nt_product(pair_w, 2 * quarter, half, pair_body(sent, BF16))
    pair_r = begin(swap(sent, row_came.at[0], 2, across))
    nt_product(pair_w, 2 * quarter, 0, pair_body(kept, F32))
    pair_r.wait_recv()

    def join_pair(rows):
        summed[rows, :] = (kept[rows, :] + row_came[0, rows, :].astype(F32)).astype(BF16)

    rows_loop(join_pair)
    pair_c = begin(swap(summed, col_came, 3, beside))
    gate_r = begin(swap(gate_grad, gate_row, 4, across))
    up_r = begin(swap(up_grad, up_row, 5, across))
    mixed_r = begin(swap(mixed_came, mixed_came_row, 6, across))

    def down_product(start, target, dtype):
        def body(j, slot):
            target[:, columns_at(j)] = mm(hidden[...], tall_tiles[slot]).astype(dtype)

        stream(
            lambda j: [down_w.at[:, pl.ds(pl.multiple_of(start + j * 256, 256), 256)]],
            lambda slot: [tall_tiles.at[slot]],
            tile_sems,
            half // 256,
            body,
        )

    pair_r.wait_send()
    pending[:] = [copy for copy in pending if copy is not pair_r]
    down_product(half, sent, BF16)
    layer_r = begin(swap(sent, row_came.at[1], 7, across))
    down_product(0, kept, F32)
    layer_r.wait_recv()

    def mine_of(value):
        return jnp.where(col == 0, value[:, :block], value[:, block:])

    def theirs_of(value):
        return jnp.where(col == 0, value[:, block:], value[:, :block])

    def join_layer(rows):
        total = kept[rows, :] + row_came[1, rows, :].astype(F32)
        layer_own[rows, :] = mine_of(total)
        block_sent[0, rows, :] = theirs_of(total).astype(BF16)

    rows_loop(join_layer)
    layer_c = begin(swap(block_sent.at[0], block_came.at[0], 8, beside))
    middle_in = pltpu.make_async_copy(middle, kept, copy_sems.at[0])
    middle_in.start()

    for copy in to_x:
        copy.wait_recv()
    for at in range(per):
        there = pl.ds(at * width, width)
        on_row.append(
            begin(
                swap(
                    hidden_came.at[:, there],
                    hidden_came_row.at[:, there],
                    2 * per + at,
                    across,
                    piece_sems,
                )
            )
        )

    def down_grad(part, left_of, came):
        def body(columns, _):
            for at in range(per):
                there = pl.ds(at * width, width)
                total = mm_tn(left_of(at)[...], top_half[:, columns])
                total = total + mm_tn(came[:, there], top_came[:, columns])
                down_grads[pl.ds((part * per + at) * width, width), columns] = total.astype(BF16)

        tiles_loop(half, 512, body)

    down_grad(0, lambda at: hidden_part(x, at), hidden_came)
    for copy in to_row + on_row:
        copy.wait_recv()
    down_grad(1, lambda at: hidden_row.at[:, pl.ds(at * width, width)], hidden_came_row)
    down_line.run(0, 1)

    middle_in.wait()
    pair_c.wait_recv()
    feed_sum[...] = jnp.zeros_like(feed_sum)

    def second_grads(rows):
        grad = summed[rows, :].astype(F32) + col_came[rows, :].astype(F32)
        return grad, grad * gain_second[...]

    def norm_first_pass(rows):
        grad, scaled = second_grads(rows)
        held = kept[rows, :]
        feed_sum[...] += jnp.sum(grad * held * inverse_second[rows, :], axis=0, keepdims=True)
        total = jnp.sum(scaled * held, axis=1, keepdims=True)
        dots[0, rows, :] = jnp.broadcast_to(total, (total.shape[0], 128))

    rows_loop(norm_first_pass)
    dot_r = begin(swap(dots.at[0], dots.at[1], 9, across))
    dot_r.wait_recv()

    def norm_second_pass(rows):
        _, scaled = second_grads(rows)
        held = kept[rows, :]
        inverse = inverse_second[rows, :]
        dot = dots[0, rows, :1] + dots[1, rows, :1]
        grad = (
            top_half[rows, :].astype(F32) + scaled * inverse - held * (inverse**3 * dot / D)
        )
        branch[rows, :] = grad.astype(BF16)
        middle_own[rows, :] = mine_of(grad)
        layer_own[rows, :] += mine_of(held)

    rows_loop(norm_second_pass)
    branch_r = begin(swap(branch, branch_row, 10, across))
    branch_r.wait_recv()

    def mixed_body(j, slot):
        total = mm_nt(branch[...], tiles[slot, :, :half])
        total = total + mm_nt(branch_row[...], tiles[slot, :, half:D])
        mixed_grad[:, columns_at(j)] = total.astype(BF16)

    stream(
        lambda j: [out_w.at[pl.ds(pl.multiple_of(j * 256, 256), 256), :]],
        lambda slot: [tiles.at[slot, :, pl.ds(0, D)]],
        tile_sems,
        out_w.shape[0] // 256,
        mixed_body,
    )
    down_line.run(1, 2)
    pairs = turned.shape[1] // 384
    lower = lax.broadcasted_iota(jnp.int32, (SL, SL), 1) <= lax.broadcasted_iota(
        jnp.int32, (SL, SL), 0
    )

    def attend(at, _):
        micro, pair = at // pairs, lax.rem(at, pairs)
        rows = pl.ds(pl.multiple_of(micro * SL, SL), SL)

        def part(kind):
            return pl.ds(pl.multiple_of(pair * 384 + kind * 128, 128), 128)

        allowed = lower & (key_live[pl.ds(micro, 1), :] > 0.5)
        dq, dk, dv = head_grads(
            turned[rows, part(0)],
            turned[rows, part(1)],
            turned[rows, part(2)],
            mixed_grad[rows, pl.ds(pl.multiple_of(pair * 128, 128), 128)],
            allowed,
            cos[...],
            first[...],
            second[...],
        )
        dqkv[rows, part(0)] = dq
        dqkv[rows, part(1)] = dk
        dqkv[rows, part(2)] = dv
        return 0

    lax.fori_loop(0, MICRO * pairs, attend, 0)

    def first_body(target, dtype):
        def body(j, slot):
            total = mm_nt(dqkv[...], tiles[slot, :, : dqkv.shape[1]])
            target[:, columns_at(j)] = total.astype(dtype)

        return body

    layer_r.wait_send()
    pending[:] = [copy for copy in pending if copy is not layer_r]
    nt_product(qkv_w, dqkv.shape[1], half, first_body(sent, BF16))
    first_r = begin(swap(sent, row_came.at[2], 11, across))
    dqkv_r = begin(swap(dqkv, dqkv_row, 12, across))
    nt_product(qkv_w, dqkv.shape[1], 0, first_body(kept, F32))
    first_r.wait_recv()

    def join_first(rows):
        total = kept[rows, :] + row_came[2, rows, :].astype(F32)
        first_own[rows, :] = mine_of(total)
        block_sent[1, rows, :] = theirs_of(total).astype(BF16)

    rows_loop(join_first)
    first_c = begin(swap(block_sent.at[1], block_came.at[1], 13, beside))
    down_line.run(2, line - 1)

    second_x.wait_recv()
    depth = second_mine.shape[0]
    turned_left[:, :depth] = second_mine[...].T
    turned_left[:, depth:] = second_came[...].T
    gate_x.wait_recv()
    gate_on = begin(swap(gate_came, gate_came_row, 14, across))

    def gate_part(shift, sources, values):
        def body(j, slot):
            mine, came = values(j, slot)
            total = mm(turned_left[:, :depth], mine) + mm(turned_left[:, depth:], came)
            there = pl.ds(pl.multiple_of(shift + j * 512, 512), 512)
            gate_grads[:, there] = total.astype(BF16)

        stream(
            lambda j: [source.at[:, columns_at(j, 512)] for source in sources],
            lambda slot: [pair_tiles.at[slot, k] for k in range(len(sources))],
            tile_sems,
            quarter // 512,
            body,
        )

    gate_part(
        0,
        [gate_came],
        lambda j, slot: (gate_grad[:, columns_at(j, 512)], pair_tiles[slot, 0]),
    )
    gate_r.wait_recv()
    gate_on.wait_recv()
    gate_part(
        quarter,
        [gate_row, gate_came_row],
        lambda j, slot: (pair_tiles[slot, 0], pair_tiles[slot, 1]),
    )

    layer_c.wait_recv()
    first_c.wait_recv()
    attention_sum[...] = jnp.zeros_like(attention_sum)

    def last_first_pass(rows):
        layer = layer_own[rows, :] + block_came[0, rows, :].astype(F32)
        both_out[rows, :] = layer.astype(BF16)
        grad = first_own[rows, :] + block_came[1, rows, :].astype(F32)
        first_own[rows, :] = grad
        held = x_own[rows, :].astype(F32)
        attention_sum[...] += jnp.sum(grad * held * inverse_first[rows, :], axis=0, keepdims=True)
        total = jnp.sum(grad * gain_first[...] * held, axis=1, keepdims=True)
        dots[2, rows, :] = jnp.broadcast_to(total, (total.shape[0], 128))

    rows_loop(last_first_pass)
    dot_r = begin(swap(dots.at[2], dots.at[3], 15, across))
    dot_r.wait_recv()

    def add_dots(rows):
        dots[4, rows, :] = dots[2, rows, :] + dots[3, rows, :]

    rows_loop(add_dots)
    dot_c = begin(swap(dots.at[4], dots.at[5], 16, beside))
    dot_c.wait_recv()

    def last_second_pass(rows):
        inverse = inverse_first[rows, :]
        dot = dots[4, rows, :1] + dots[5, rows, :1]
        scaled = first_own[rows, :] * gain_first[...]
        held = x_own[rows, :].astype(F32)
        grad = middle_own[rows, :] + scaled * inverse - held * (inverse**3 * dot / D)
        below = pl.ds(pl.multiple_of(rows.start + ROWS, rows.size), rows.size)
        both_out[below, :] = grad.astype(BF16)

    rows_loop(last_second_pass)
    pieces_out[0:1, :] = attention_sum[...]
    pieces_out[1:2, :] = mine_of(feed_sum[...])

    down_line.stage = kept.at[pl.ds(0, down_grads.shape[0] // line), :]
    down_line.finish()
    down_store = pltpu.make_async_copy(down_line.stage, down_out, copy_sems.at[1])
    down_store.start()
    for copy in (up_r, mixed_r, dqkv_r):
        copy.wait_recv()
    for copy in pending:
        copy.wait_send()
    down_store.wait()


def chain(line, identity, *values):
    hidden, gate_grad = values[:2]
    quarter = hidden.shape[1]
    narrow = values[3].shape[1]
    mixed_width = values[7].shape[1]
    qkv_width = values[12].shape[1]
    half, block = D // 2, D // 4
    rows = quarter // 2
    vmem = pl.BlockSpec(memory_space=pltpu.VMEM)
    anywhere = pl.BlockSpec(memory_space=pl.ANY)
    outside = {8, 9, 10, 11, 13}

    def array(*shape, dtype=BF16):
        return jax.ShapeDtypeStruct(shape, dtype)

    def buffer(*shape, dtype=BF16):
        return pltpu.VMEM(shape, dtype)

    outs = [
        (array(2 * rows // line, half, dtype=F32), anywhere),
        (array(narrow, 2 * quarter), vmem),
        (array(ROWS, narrow), vmem),
        (array(ROWS, quarter), anywhere),
        (array(ROWS, qkv_width), vmem),
        (array(ROWS, qkv_width), anywhere),
        (array(ROWS, half), vmem),
        (array(ROWS, mixed_width), anywhere),
        (array(2 * ROWS, block), vmem),
        (array(2, block, dtype=F32), vmem),
        (array(ROWS, quarter), anywhere),
        (array(ROWS, quarter), anywhere),
        (array(ROWS, quarter), anywhere),
    ]
    sem = pltpu.SemaphoreType.DMA
    return pl.pallas_call(
        lambda *refs: chain_kernel(line, *refs),
        out_shape=[shape for shape, _ in outs],
        in_specs=[anywhere if k in outside else vmem for k in range(len(values))],
        out_specs=[place for _, place in outs],
        scratch_shapes=[
            buffer(2, 256, 2 * quarter),
            buffer(2, quarter, 256),
            buffer(2, 2, ROWS, 512),
            buffer(ROWS, half, dtype=F32),
            buffer(ROWS, half),
            buffer(3, ROWS, half),
            buffer(ROWS, half),
            buffer(ROWS, half),
            buffer(2, ROWS, block),
            buffer(2, ROWS, block),
            buffer(ROWS, rows),
            buffer(ROWS, rows),
            buffer(ROWS, rows),
            buffer(ROWS, half),
            buffer(6, ROWS, 128, dtype=F32),
            buffer(2 * rows, half),
            buffer(2, line - 1, 2 * rows // line, half),
            buffer(ROWS, block, dtype=F32),
            buffer(ROWS, block, dtype=F32),
            buffer(ROWS, block, dtype=F32),
            buffer(ROWS, qkv_width // 3),
            buffer(narrow, 2 * ROWS),
            buffer(1, half, dtype=F32),
            buffer(1, block, dtype=F32),
            sem((2, 17)),
            sem((2, 3 * (line // 2))),
            sem((2, 2)),
            sem((2, 2, line - 1, 4)),
            sem((2,)),
        ],
        compiler_params=pltpu.CompilerParams(
            collective_id=identity, has_side_effects=True, vmem_limit_bytes=67043328
        ),
        cost_estimate=FREE,
    )(*values)


def tail_sums(line, identity, *values):
    (gate_grads, up, _, _, _, dqkv, _, _, _, branch) = values[:10]
    rows = gate_grads.shape[0]
    side_rows = 2 * values[10].shape[1]
    tokens = up.shape[0]
    widths = (gate_grads.shape[1], gate_grads.shape[1], 2 * dqkv.shape[1], branch.shape[1])
    heights = (rows, rows, rows, side_rows)
    pieces = (4, 4, 3, 1)
    sizes = [(h // line, w) for h, w in zip(heights, widths)]
    vmem = pl.BlockSpec(memory_space=pltpu.VMEM)
    anywhere = pl.BlockSpec(memory_space=pl.ANY)
    both, gains = values[14:]
    height = sizes[0][0]
    gain_steps = both.shape[1].bit_length() - 1

    def buffer(*shape):
        return pltpu.VMEM(shape, BF16)

    def array(*shape):
        return jax.ShapeDtypeStruct(shape, F32)

    return pl.pallas_call(
        lambda *refs: tail_kernel(line, *refs),
        out_shape=[
            array(*sizes[0]),
            array(*sizes[1]),
            array(height, widths[2] // 3),
            array(height, widths[2] // 3),
            array(height, widths[2] // 3),
            array(*sizes[3]),
            jax.ShapeDtypeStruct(both.shape, BF16),
            array(*gains.shape),
        ],
        in_specs=[vmem] * 14 + [anywhere, vmem],
        out_specs=[anywhere] * 7 + [vmem],
        scratch_shapes=[buffer(2, line - 1, *size) for size in sizes]
        + [buffer(h, w) for h, w in zip(heights[1:], widths[1:])]
        + [buffer(*up.shape)] * 2
        + [buffer(*dqkv.shape)] * 2
        + [buffer(*branch.shape)]
        + [buffer(rows, 2 * tokens)]
        + [pltpu.VMEM(size, F32) for size in sizes]
        + [pltpu.SemaphoreType.DMA((2, 2, line - 1, count)) for count in pieces]
        + [pltpu.SemaphoreType.DMA((2, 5)), pltpu.SemaphoreType.DMA((6 + widths[2] // 128,))]
        + [pltpu.VMEM((2, gain_steps, *gains.shape), F32)]
        + [
            pltpu.SemaphoreType.DMA((2, both.shape[1])),
            pltpu.SemaphoreType.DMA((2, gain_steps)),
        ],
        compiler_params=pltpu.CompilerParams(
            collective_id=identity, has_side_effects=True, vmem_limit_bytes=67043328
        ),
        cost_estimate=FREE,
    )(*values)


def put_back_kernel(order_ref, back_ref, layer_ref, grad_ref):
    groups = back_ref.shape[1]

    def one(at, _):
        micro, slot = at // groups, lax.rem(at, groups)
        place = order_ref[micro, slot]
        layer_ref[micro, place] = back_ref[micro, slot]
        grad_ref[micro, place] = back_ref[MICRO + micro, slot]
        return 0

    lax.fori_loop(0, MICRO * groups, one, 0)


def put_back(order, back):
    vmem = pl.BlockSpec(memory_space=pltpu.VMEM)
    shape = jax.ShapeDtypeStruct((MICRO,) + back.shape[1:], BF16)
    return pl.pallas_call(
        put_back_kernel,
        out_shape=(shape, shape),
        in_specs=[pl.BlockSpec(memory_space=pltpu.SMEM), vmem],
        out_specs=(vmem, vmem),
        cost_estimate=FREE,
    )(order, back)


def per_device(
    tokens,
    lengths,
    deal_order,
    attention_gain,
    query_weight,
    key_weight,
    value_weight,
    output_weight,
    feed_gain,
    gate_weight,
    up_weight,
    down_weight,
    cotangent,
):
    groups = lax.axis_size("dp")
    line = groups // 2
    dp = lax.axis_index("dp")
    row = lax.axis_index("row")
    col = lax.axis_index("col")
    z, x = dp // 2, dp % 2
    half = D // 2
    block = D // 4

    def over_row(v):
        return lax.ppermute(v, "row", SWAP)

    def over_col(v):
        return lax.ppermute(v, "col", SWAP)

    def over_x(v):
        return lax.ppermute(v, "dp", [(i, i ^ 1) for i in range(groups)])

    def ordered(own, other, index, axis=-1):
        return jnp.where(
            index == 0,
            jnp.concatenate([own, other], axis=axis),
            jnp.concatenate([other, own], axis=axis),
        )

    def x_parts(v, width):
        even = jnp.concatenate(
            [v[:, s : s + width] for s in range(0, v.shape[1], 2 * width)], axis=1
        )
        odd = jnp.concatenate(
            [v[:, s : s + width] for s in range(width, v.shape[1], 2 * width)], axis=1
        )
        return jnp.where(x == 0, even, odd), jnp.where(x == 0, odd, even)

    token = []

    def ordered_after(*values):
        out = lax.optimization_barrier(tuple(values) + tuple(token))
        return out[: len(values)] if len(values) > 1 else out[0]

    def mark(value):
        token[:] = [value]
        return value

    def arrive(*values):
        out = ordered_after(*values)
        mark(out[0] if len(values) > 1 else out)
        return out

    gathered = jnp.take_along_axis(tokens, deal_order[:, :, None, None], axis=1)
    gathered = mark(lax.optimization_barrier(gathered))
    dealt = lax.all_to_all(gathered, "dp", split_axis=1, concat_axis=2, tiled=True)
    own_order = lax.dynamic_slice_in_dim(deal_order, dp, 1, 1)
    own_lengths = jnp.take_along_axis(lengths, own_order, axis=1)[:, 0]
    tables = rope_tables()
    live = (jnp.arange(SL, dtype=jnp.int32)[None, :] < own_lengths[:, None]).reshape(ROWS, 1)
    key_live = live.reshape(MICRO, SL).astype(F32)
    top_block = jnp.where(live, cotangent.reshape(ROWS, block), 0.0).astype(BF16)

    gains = jnp.stack([attention_gain, feed_gain])
    gains_half = ordered(gains, over_col(gains), col)
    gains_other = over_row(gains_half)
    gains_full = jnp.concatenate([gains_half, gains_other], axis=1)

    top_col = over_col(top_block)
    quarter = gate_weight.shape[1] // 2
    gate_weight, up_weight = ordered_after(gate_weight, up_weight)
    (pair_w,) = swap_weights(
        (gate_weight, up_weight),
        ((0, False, 0, 0, 0, quarter), (1, False, 0, 0, quarter, quarter)),
        ((D, 2 * quarter),),
        0,
    )
    mark(pair_w)
    x_block = arrive(dealt).reshape(ROWS, block)
    x_came = over_col(x_block)
    heads = query_weight.shape[1] // 2
    query_weight, key_weight, value_weight, output_weight = ordered_after(
        query_weight, key_weight, value_weight, output_weight
    )
    plan = [
        (kind, False, 0, at, 3 * at + 128 * kind, 128)
        for kind in range(3)
        for at in range(0, heads, 128)
    ]
    qkv_w, out_w = swap_weights(
        (query_weight, key_weight, value_weight, output_weight),
        tuple(plan) + ((3, True, 1, 0, 0, heads),),
        ((D, 3 * heads), (heads, D)),
        1,
    )
    mark(qkv_w)
    top_half = ordered(top_block, arrive(top_col), col)
    top_half = mark(lax.optimization_barrier(top_half))
    x_half = ordered(x_block, arrive(x_came), col)
    x_half = mark(lax.optimization_barrier(x_half))
    top_came = over_x(top_half)
    top_row = over_row(top_half)

    x_other = arrive(over_row(x_half))
    x_full = jnp.concatenate([x_half, x_other], axis=1).astype(F32)
    inverse_first = lax.rsqrt(jnp.mean(x_full * x_full, axis=1, keepdims=True) + EPSILON)
    normed_first = (x_full * inverse_first * gains_full[0][None, :]).astype(BF16)
    normed_first = mark(lax.optimization_barrier(normed_first))
    qkv = multiply(normed_first, qkv_w, False, 384, F32)
    mixed, turned = attend_forward(own_lengths, qkv, tables)
    kept, sent = split_product([mixed], out_w, False, 512)
    mark(sent)
    came = arrive(over_row(sent))
    summed = (kept + came.astype(F32)).astype(BF16)
    summed = mark(lax.optimization_barrier(summed))
    summed_other = over_col(summed)
    top_row = arrive(top_row)
    narrow = half // groups
    first_mine, first_theirs = x_parts(normed_first[:, :half], narrow)
    top_full = jnp.concatenate([top_half, top_row], axis=1)
    (down_w,) = swap_weights(
        (ordered_after(down_weight),),
        ((0, True, 0, 0, 0, down_weight.shape[0] // 2),),
        ((down_weight.shape[0] // 2, D),),
        2,
    )
    hidden_grad = mark(multiply(top_full, down_w, True, 512, F32))
    top_came = arrive(top_came)
    mixed_mine, mixed_theirs = x_parts(mixed, 2 * mixed.shape[1] // groups)
    first_came = over_x(ordered_after(first_theirs))
    mixed_came = over_x(ordered_after(mixed_theirs))
    mixed_row = over_row(mixed_mine)
    summed_other = arrive(summed_other)
    middle = x_half.astype(F32) + (summed.astype(F32) + summed_other.astype(F32))

    middle_low = middle.astype(BF16)
    middle_low, middle = lax.optimization_barrier((middle_low, middle))
    mark(middle_low)
    middle_other = arrive(over_row(middle_low))
    middle_full = jnp.concatenate([middle_low, middle_other], axis=1).astype(F32)
    inverse_second = lax.rsqrt(
        jnp.mean(middle_full * middle_full, axis=1, keepdims=True) + EPSILON
    )
    normed_second = (middle_full * inverse_second * gains_full[1][None, :]).astype(BF16)
    normed_second = mark(lax.optimization_barrier(normed_second))
    hidden, gate_grad, up_grad = feed_forward(normed_second, pair_w, hidden_grad)
    mark(hidden)
    first_came, mixed_came, mixed_row = arrive(first_came, mixed_came, mixed_row)

    def own_block(v):
        return lax.dynamic_slice_in_dim(v, col * block, block, 1)

    second_mine, second_theirs = x_parts(normed_second[:, :half], narrow)
    (
        down_sum,
        gate_grads,
        second_came,
        up_row,
        dqkv,
        dqkv_row,
        branch,
        mixed_came_row,
        both,
        pieces,
        _,
        _,
        _,
    ) = chain(
        line,
        4,
        *ordered_after(
            hidden,
            gate_grad,
            up_grad,
            second_mine,
            second_theirs,
            top_half,
            top_came,
            mixed_came,
            pair_w,
            down_w,
            qkv_w,
            out_w,
            turned,
            middle,
            inverse_first,
            inverse_second,
            gains_half[1:],
            own_block(gains_half)[:1],
            x_block,
            key_live,
            *tables,
        ),
    )
    mark(both)

    gate_sum, up_sum, query_sum, key_sum, value_sum, output_sum, back, gain_sums = tail_sums(
        line,
        3,
        *ordered_after(
            gate_grads,
            up_grad,
            up_row,
            second_mine,
            second_came,
            dqkv,
            dqkv_row,
            first_mine,
            first_came,
            branch,
            mixed_mine,
            mixed_came,
            mixed_row,
            mixed_came_row,
            both.reshape(2 * MICRO, groups, SL // groups, block),
            pieces,
        ),
    )
    layer_output, tokens_grad = put_back(deal_order, back)
    gain_size = block // groups
    gain_sums = lax.dynamic_slice_in_dim(gain_sums, dp * gain_size, gain_size, 1)

    return (
        layer_output,
        tokens_grad,
        gain_sums[0],
        query_sum,
        key_sum,
        value_sum,
        output_sum,
        gain_sums[1],
        gate_sum,
        up_sum,
        down_sum,
    )


def solution(mesh):
    in_specs = (
        P(None, None, "dp", ("row", "col")),
        P(),
        P(),
        P(("row", "col")),
        P("row", "col"),
        P("row", "col"),
        P("row", "col"),
        P("col", "row"),
        P(("row", "col")),
        P("row", "col"),
        P("row", "col"),
        P("col", "row"),
        P(None, "dp", None, ("row", "col")),
    )
    out_specs = (
        P(None, None, "dp", ("row", "col")),
        P(None, None, "dp", ("row", "col")),
        P(("row", "col", "dp")),
        P(("row", "dp"), "col"),
        P(("row", "dp"), "col"),
        P(("row", "dp"), "col"),
        P(("col", "dp"), "row"),
        P(("row", "col", "dp")),
        P(("row", "dp"), "col"),
        P(("row", "dp"), "col"),
        P(("col", "dp"), "row"),
    )
    return jax.shard_map(
        per_device, mesh=mesh, in_specs=in_specs, out_specs=out_specs, check_vma=False
    )
```

profile of v0, /device:TPU:0, one launch (start us, length us, event | category | flops | bytes accessed | tf_op | source)
XLA Modules:
  0.0 499.3 jit_solution(10830590816014199140)
XLA Ops:
  2.1 1.7 gather_fusion
  4.7 7.3 %all-to-all-start = ((bf16[2,8,32,512]{3,2,0,1:T(8,128)(2,1)}), bf16[2,8,32,512]{3,2,0,1:T(8,128)(2,1)S(1)}, u32[]{:S(2)}, u32[]{:S(2)}) async-start(bf16[2,8,32,512]{3,2,0,1:T(8,128)(2,1)} %copy.35), calls=%async_computation | async-start | bytes 1048576 | tf_op jit(solution)/shard_map/all_to_all | solution.py:1337
  15.8 13.6 %shard_map.212.gate_ref.up_ref.refs_8_ = bf16[2048,4096]{1,0:T(8,128)(2,1)} custom-call(bf16[1024,4096]{1,0:T(8,128)(2,1)} %refs_0_, bf16[1024,4096]{1,0:T(8,128)(2,1)} %refs_1_), custom_call_target="tpu_custom_call" | custom-call | tf_op jit(solution)/shard_map/pallas_call | solution.py:317
  30.1 8.0 %shard_map.213 = (bf16[2048,1536]{1,0:T(8,128)(2,1)}, bf16[512,2048]{1,0:T(8,128)(2,1)}) custom-call(bf16[1024,1024]{1,0:T(8,128)(2,1)} %refs_0_.1, bf16[1024,1024]{1,0:T(8,128)(2,1)} %refs_1_.1, bf16[1024,1024]{1,0:T(8,128)(2,1)} %refs_2_, bf16[1024,1024]{1,0:T(8,128)(2,1)} %refs_3_), custom_call_target="tpu_custom_call" | custom-call | tf_op jit(solution)/shard_map/pallas_call | solution.py:317
  38.4 5.2 %collective-permute-done = bf16[512,512]{1,0:T(8,128)(2,1)} collective-permute-done((bf16[512,512]{1,0:T(8,128)(2,1)S(1)}, bf16[512,512]{1,0:T(8,128)(2,1)}, u32[]{:S(2)}, u32[]{:S(2)}) %collective-permute-start) | collective-permute-done | bytes 524320 | tf_op jit(solution)/shard_map/ppermute | solution.py:1299
  50.7 1.9 fusion.2.a_ref
  52.6 8.6 %shard_map.214.qkv_ref = f32[512,1536]{1,0:T(8,128)} custom-call(bf16[512,2048]{1,0:T(8,128)(2,1)} %fusion.2.a_ref, bf16[2048,1536]{1,0:T(8,128)(2,1)} %get-tuple-element.143.w_ref.refs_10_), custom_call_target="tpu_custom_call" | custom-call | tf_op jit(solution)/shard_map/pallas_call | solution.py:169
  61.3 9.0 %shard_map.215 = (bf16[512,512]{1,0:T(8,128)(2,1)}, bf16[512,1536]{1,0:T(8,128)(2,1)}) custom-call(s32[2]{0:T(128)} %copy-done.16, f32[512,1536]{1,0:T(8,128)} %shard_map.214.qkv_ref, f32[256,128]{1,0:T(8,128)} %pad_maximum_fusion.9.cos_ref.refs_20_, f32[256,128]{1,0:T(8,128)} %get-tuple-element.154.first_ref.refs_21_, ...), custom_call_target="tpu_custom_call" | custom-call | tf_op jit(solution)/shard_map/pallas_call | solution.py:141
  70.2 5.2 %shard_map.216 = (f32[512,1024]{1,0:T(8,128)}, bf16[512,1024]{1,0:T(8,128)(2,1)}) custom-call(bf16[512,512]{1,0:T(8,128)(2,1)} %get-tuple-element.113.refs_0_, bf16[512,2048]{1,0:T(8,128)(2,1)} %get-tuple-element.144.refs_1_.refs_11_), custom_call_target="tpu_custom_call" | custom-call | tf_op jit(solution)/shard_map/pallas_call | solution.py:207
  76.0 2.0 collective-permute-start.7
  78.3 2.0 add_convert_fusion
  80.9 7.5 %shard_map.217.w_ref.refs_9_ = bf16[2048,2048]{1,0:T(8,128)(2,1)} custom-call(bf16[4096,1024]{1,0:T(8,128)(2,1)} %refs_0_.2), custom_call_target="tpu_custom_call" | custom-call | tf_op jit(solution)/shard_map/pallas_call | solution.py:317
  88.5 2.8 pad_maximum_fusion.1.a_ref
  91.2 9.3 %shard_map.218.da_ref = f32[512,2048]{1,0:T(8,128)} custom-call(bf16[512,2048]{1,0:T(8,128)(2,1)} %pad_maximum_fusion.1.a_ref, bf16[2048,2048]{1,0:T(8,128)(2,1)} %shard_map.217.w_ref.refs_9_), custom_call_target="tpu_custom_call" | custom-call | tf_op jit(solution)/shard_map/pallas_call | solution.py:169
  101.6 4.2 collective-permute-done.6
  105.7 3.2 fusion.12
  114.0 2.0 collective-permute-start.11
  116.0 1.7 fusion.3
  117.7 3.1 fusion.5.x_ref
  120.8 17.2 %shard_map.219 = (bf16[512,2048]{1,0:T(8,128)(2,1)}, bf16[512,2048]{1,0:T(8,128)(2,1)}, bf16[512,2048]{1,0:T(8,128)(2,1)}) custom-call(bf16[512,2048]{1,0:T(8,128)(2,1)} %fusion.5.x_ref, bf16[2048,4096]{1,0:T(8,128)(2,1)} %shard_map.212.gate_ref.up_ref.refs_8_, bf16[2048,4096]{1,0:T(8,128)(2,1)} %shard_map.212.gate_ref.up_ref.refs_8_, ...), custom_call_target="tpu_custom_call" | custom-call | tf_op jit(solution)/shard_map/pallas_call | solution.py:241
  141.3 112.1 %shard_map.220 = (f32[512,1024]{1,0:T(8,128)}, bf16[512,4096]{1,0:T(8,128)(2,1)}, bf16[512,512]{1,0:T(8,128)(2,1)}, bf16[512,2048]{1,0:T(8,128)(2,1)}, bf16[512,...) custom-call(bf16[512,2048]{1,0:T(8,128)(2,1)} %get-tuple-element.133, ...), custom_call_target="tpu_custom_call" | custom-call | tf_op jit(solution)/shard_map/pallas_call | solution.py:1147
  253.4 231.6 %shard_map.221 = (f32[128,4096]{1,0:T(8,128)}, f32[128,4096]{1,0:T(8,128)}, f32[128,1024]{1,0:T(8,128)}, f32[128,1024]{1,0:T(8,128)}, f32[128,1024]{1,0:T(8,128)...) custom-call(bf16[512,4096]{1,0:T(8,128)(2,1)} %get-tuple-element.166.refs_0_, ...), custom_call_target="tpu_custom_call" | custom-call | tf_op jit(solution)/shard_map/pallas_call | solution.py:1211
  485.1 2.6 shard_map.222
  488.9 2.0 copy.48
  (105 shorter events, 34.6 us)
Async XLA Ops:
  2.1 9.9 %copy-start.13 = (s32[2,8]{1,0:T(2,128)S(1)}, s32[2,8]{1,0:T(2,128)}, u32[]{:S(2)}) copy-start(s32[2,8]{1,0:T(2,128)} %order_ref.1) | copy-start | bytes 196
  2.1 10.4 %copy-start = (s32[2,8]{1,0:T(2,128)S(1)}, s32[2,8]{1,0:T(2,128)}, u32[]{:S(2)}) copy-start(s32[2,8]{1,0:T(2,128)} %param.14) | copy-start | bytes 196
  3.8 10.3 %copy-start.12 = (bf16[2,1,256,512]{3,2,1,0:T(8,128)(2,1)S(1)}, bf16[2,1,256,512]{3,2,1,0:T(8,128)(2,1)}, u32[]{:S(2)}) copy-start(bf16[2,1,256,512]{3,2,1,0:T(8,128)(2,1)} %param.25) | copy-start | bytes 1572868
  4.7 24.7 %all-to-all-start = ((bf16[2,8,32,512]{3,2,0,1:T(8,128)(2,1)}), bf16[2,8,32,512]{3,2,0,1:T(8,128)(2,1)S(1)}, u32[]{:S(2)}, u32[]{:S(2)}) async-start(bf16[2,8,32,512]{3,2,0,1:T(8,128)(2,1)} %copy.35), calls=%async_computation | async-start | bytes 1048576 | tf_op jit(solution)/shard_map/all_to_all | solution.py:1337
  13.4 16.0 %copy-start.16 = (s32[2]{0:T(128)}, s32[2]{0:T(128)S(1)}, u32[]{:S(2)}) copy-start(s32[2]{0:T(128)S(1)} %fusion.9.len_ref) | copy-start | bytes 28
  14.2 23.8 %collective-permute-start.1 = (bf16[512,512]{1,0:T(8,128)(2,1)S(1)}, bf16[512,512]{1,0:T(8,128)(2,1)S(1)}, u32[]{:S(2)}, u32[]{:S(2)}) collective-permute-start(bf16[512,512]{1,0:T(8,128)(2,1)S(1)} %bitcast_select_fusion), channel_id=1, source_target_pairs={{0,1},{1,0},{2,3},{3,2},{4,5},{5,4},{6,7},{7,6},{8,9},{9,8},{10,11... | collective-permute-start | bytes 1572872 | tf_op jit(solution)/shard_map/ppermute | solution.py:1299
  29.5 14.2 %copy-start.4 = (bf16[2,8,32,512]{3,2,1,0:T(8,128)(2,1)}, bf16[2,8,32,512]{3,2,1,0:T(8,128)(2,1)S(1)}, u32[]{:S(2)}) copy-start(bf16[2,8,32,512]{3,2,1,0:T(8,128)(2,1)S(1)} %copy.36) | copy-start | bytes 1572868
  29.5 14.1 %collective-permute-start = (bf16[512,512]{1,0:T(8,128)(2,1)S(1)}, bf16[512,512]{1,0:T(8,128)(2,1)}, u32[]{:S(2)}, u32[]{:S(2)}) collective-permute-start(bf16[512,512]{1,0:T(8,128)(2,1)S(1)} %bitcast.23), channel_id=1, source_target_pairs={{0,1},{1,0},{2,3},{3,2},{4,5},{5,4},{6,7},{7,6},{8,9},{9,8},{10,11... | collective-permute-start | bytes 1572872 | tf_op jit(solution)/shard_map/ppermute | solution.py:1299
  38.0 7.2 %copy-start.14 = (f32[512]{0:T(512)S(1)}, f32[512]{0:T(512)}, u32[]{:S(2)}) copy-start(f32[512]{0:T(512)} %param.21) | copy-start | bytes 6148
  38.0 7.2 %copy-start.15 = (f32[512]{0:T(512)S(1)}, f32[512]{0:T(512)}, u32[]{:S(2)}) copy-start(f32[512]{0:T(512)} %param.16) | copy-start | bytes 6148
  38.4 50.1 %copy-start.3 = (bf16[512,1024]{1,0:T(8,128)(2,1)}, bf16[512,1024]{1,0:T(8,128)(2,1)S(1)}, u32[]{:S(2)}) copy-start(bf16[512,1024]{1,0:T(8,128)(2,1)S(1)} %maximum_select_fusion.refs_5_) | copy-start | bytes 3145732
  45.2 5.1 %collective-permute-start.2 = (bf16[512,1024]{1,0:T(8,128)(2,1)S(1)}, bf16[512,1024]{1,0:T(8,128)(2,1)S(1)}, u32[]{:S(2)}, u32[]{:S(2)}) collective-permute-start(bf16[512,1024]{1,0:T(8,128)(2,1)S(1)} %maximum_select_fusion.1), channel_id=1, source_target_pairs={{0,2},{2,0},{1,3},{3,1},{4,6},{6,4},{5,7},{7,5},{8,10},{10,8},{9,1... | collective-permute-start | bytes 3145736 | tf_op jit(solution)/shard_map/ppermute | solution.py:1296
  45.3 3.7 collective-permute-start.3
  49.0 1.2 collective-permute-start.4
  75.5 2.9 collective-permute-start.5
  75.6 5.3 %collective-permute-start.8 = (bf16[512,1024]{1,0:T(8,128)(2,1)S(1)}, bf16[512,1024]{1,0:T(8,128)(2,1)}, u32[]{:S(2)}, u32[]{:S(2)}) collective-permute-start(bf16[512,1024]{1,0:T(8,128)(2,1)S(1)} %maximum_select_fusion.refs_5_), channel_id=1, source_target_pairs={{0,2},{2,0},{1,3},{3,1},{4,6},{6,4},{5,7},{7,5},{8,10},{10,8},{9,1... | collective-permute-start | bytes 3145736 | tf_op jit(solution)/shard_map/ppermute | solution.py:1296
  76.0 25.6 %collective-permute-start.7 = (bf16[512,1024]{1,0:T(8,128)(2,1)S(1)}, bf16[512,1024]{1,0:T(8,128)(2,1)}, u32[]{:S(2)}, u32[]{:S(2)}) collective-permute-start(bf16[512,1024]{1,0:T(8,128)(2,1)S(1)} %maximum_select_fusion.refs_5_), channel_id=1, source_target_pairs={{0,4},{4,0},{8,12},{12,8},{16,20},{20,16},{24,28},{28,24},{1,5},{5... | collective-permute-start | bytes 3145736 | tf_op jit(solution)/shard_map/ppermute | solution.py:1302
  80.3 25.4 %collective-permute-start.6 = (bf16[512,1024]{1,0:T(8,128)(2,1)S(1)}, bf16[512,1024]{1,0:T(8,128)(2,1)}, u32[]{:S(2)}, u32[]{:S(2)}) collective-permute-start(bf16[512,1024]{1,0:T(8,128)(2,1)S(1)} %add_convert_fusion), channel_id=1, source_target_pairs={{0,1},{1,0},{2,3},{3,2},{4,5},{5,4},{6,7},{7,6},{8,9},{9,8},{10,11... | collective-permute-start | bytes 3145736 | tf_op jit(solution)/shard_map/ppermute | solution.py:1299
  109.0 7.1 %collective-permute-start.9 = (bf16[512,1024]{1,0:T(8,128)(2,1)S(1)}, bf16[512,1024]{1,0:T(8,128)(2,1)}, u32[]{:S(2)}, u32[]{:S(2)}) collective-permute-start(bf16[512,1024]{1,0:T(8,128)(2,1)S(1)} %get-tuple-element.122), channel_id=1, source_target_pairs={{0,2},{2,0},{1,3},{3,1},{4,6},{6,4},{5,7},{7,5},{8,10},{10,8},{9,1... | collective-permute-start | bytes 3145736 | tf_op jit(solution)/shard_map/ppermute | solution.py:1296
  112.1 26.1 %collective-permute-start.12 = (bf16[512,256]{1,0:T(8,128)(2,1)S(1)}, bf16[512,256]{1,0:T(8,128)(2,1)}, u32[]{:S(2)}, u32[]{:S(2)}) collective-permute-start(bf16[512,256]{1,0:T(8,128)(2,1)S(1)} %get-tuple-element.176.refs_10_), channel_id=1, source_target_pairs={{0,2},{2,0},{1,3},{3,1},{4,6},{6,4},{5,7},{7,5},{8,10},{10,8},{9,1... | collective-permute-start | bytes 786440 | tf_op jit(solution)/shard_map/ppermute | solution.py:1296
  114.0 24.3 %collective-permute-start.11 = (bf16[512,256]{1,0:T(8,128)(2,1)}, bf16[512,256]{1,0:T(8,128)(2,1)}, u32[]{:S(2)}, u32[]{:S(2)}) collective-permute-start(bf16[512,256]{1,0:T(8,128)(2,1)} %get-tuple-element.128), channel_id=1, source_target_pairs={{0,4},{4,0},{8,12},{12,8},{16,20},{20,16},{24,28},{28,24},{1,5},{5... | collective-permute-start | bytes 786440 | tf_op jit(solution)/shard_map/ppermute | solution.py:1302
  116.0 22.3 %collective-permute-start.10 = (bf16[512,512]{1,0:T(8,128)(2,1)S(1)}, bf16[512,512]{1,0:T(8,128)(2,1)}, u32[]{:S(2)}, u32[]{:S(2)}) collective-permute-start(bf16[512,512]{1,0:T(8,128)(2,1)S(1)} %get-tuple-element.127), channel_id=1, source_target_pairs={{0,4},{4,0},{8,12},{12,8},{16,20},{20,16},{24,28},{28,24},{1,5},{5... | collective-permute-start | bytes 1572872 | tf_op jit(solution)/shard_map/ppermute | solution.py:1302
  120.8 17.2 %copy-start.1 = (bf16[512,2048]{1,0:T(8,128)(2,1)S(1)}, bf16[512,2048]{1,0:T(8,128)(2,1)}, u32[]{:S(2)}) copy-start(bf16[512,2048]{1,0:T(8,128)(2,1)} %fusion.5.x_ref) | copy-start | bytes 6291460
  485.1 7.4 %copy-start.9 = (f32[128,1024]{1,0:T(8,128)S(1)}, f32[128,1024]{1,0:T(8,128)}, u32[]{:S(2)}) copy-start(f32[128,1024]{1,0:T(8,128)} %get-tuple-element.248) | copy-start | bytes 1572868
  (7 other events, 27.2 us)
where the time goes:
time: 501 us; the launch traced here: 499 us
  Pallas kernels  425 us (85%)
  other arithmetic  25.5 us (5%)
  local copies, waits for them, and re-layouts  19.6 us (4%)
  starting transfers between devices  15.8 us (3%)
  waiting for transfers between devices  12.8 us (3%)
    pallas_call x1, Pallas kernels, tail_sums(): pl.pallas_call(lambda *refs: tail_kernel(line, *refs), out_shape=[array(*...  232 us
    pallas_call x1, Pallas kernels, chain(): pl.pallas_call(lambda *refs: chain_kernel(line, *refs), out_shape=[shape...  112 us
    pallas_call x3, Pallas kernels, swap_weights(): pl.pallas_call(lambda *refs: swap_kernel(plan, len(weights), len(shapes),...  29.1 us
    pallas_call x2, Pallas kernels, multiply(): pl.pallas_call(kernel, out_shape=jax.ShapeDtypeStruct((height, width), dt...  17.9 us
    pallas_call x1, Pallas kernels, feed_forward(): pl.pallas_call(feed_kernel, out_shape=(jax.ShapeDtypeStruct((height, widt...  17.2 us
    ppermute x4, waiting for transfers between devices, over_col(): return lax.ppermute(v, 'col', SWAP)  11 us
    unnamed x42, local copies, waits for them, and re-layouts  10.5 us
  transfers between devices with their start and end apart: 14, of which 6 were waited for; matrix products, arithmetic and copies ran while one was open for 4% of the time, Pallas kernels for 11%

commit v1 on v0

--- a/solution.py
+++ b/solution.py
@@ -73,35 +73,23 @@
     return exps / jnp.sum(exps, axis=1, keepdims=True)
 
 
-def allowed_of(length):
-    query = lax.broadcasted_iota(jnp.int32, (SL, SL), 0)
-    key = lax.broadcasted_iota(jnp.int32, (SL, SL), 1)
-    return (key <= query) & (key < length)
-
-
 FREE = pl.CostEstimate(flops=0, bytes_accessed=0, transcendentals=0)
-BUSY = pl.CostEstimate(flops=20 * 10**9, bytes_accessed=60 * 10**6, transcendentals=0)
 
 
 def whole(shape):
     return pl.BlockSpec(shape, lambda *at: (0,) * len(shape), pipeline_mode=pl.Buffered(1))
 
 
-def attend_kernel(len_ref, qkv_ref, cos_ref, first_ref, second_ref, o_ref, turned_ref):
-    cos, first, second = cos_ref[...], first_ref[...], second_ref[...]
-    qr = turn(qkv_ref[:, :128], cos, first, second).astype(BF16)
-    kr = turn(qkv_ref[:, 128:256], cos, first, second).astype(BF16)
-    vr = qkv_ref[:, 256:].astype(BF16)
-    turned_ref[:, :128] = qr
-    turned_ref[:, 128:256] = kr
-    turned_ref[:, 256:] = vr
-    allowed = allowed_of(len_ref[pl.program_id(0)])
+def head_outputs(qkv, allowed, cos, first, second):
+    qr = turn(qkv[:, :128], cos, first, second).astype(BF16)
+    kr = turn(qkv[:, 128:256], cos, first, second).astype(BF16)
+    vr = qkv[:, 256:].astype(BF16)
     out = jnp.zeros((SL, 128), F32)
     for head in range(2):
         mask = head_mask(head)
         probs = softmax_of(jnp.where(mask, qr, jnp.zeros_like(qr)), kr, allowed).astype(BF16)
         out = out + mm(probs, jnp.where(mask, vr, jnp.zeros_like(vr)))
-    o_ref[...] = out.astype(BF16)
+    return qr, kr, vr, out.astype(BF16)
 
 
 def head_grads(qr, kr, vr, od, allowed, cos, first, second):
@@ -129,98 +117,6 @@
     )
 
 
-def pair_block(width):
-    return pl.BlockSpec((SL, width), lambda m, h, lens: (m, h))
-
-
-TABLE = pl.BlockSpec((SL, 128), lambda m, h, lens: (0, 0))
-
-
-def attend_forward(lengths, qkv, tables):
-    width = qkv.shape[1]
-    return pl.pallas_call(
-        attend_kernel,
-        out_shape=(
-            jax.ShapeDtypeStruct((ROWS, width // 3), BF16),
-            jax.ShapeDtypeStruct((ROWS, width), BF16),
-        ),
-        grid_spec=pltpu.PrefetchScalarGridSpec(
-            num_scalar_prefetch=1,
-            grid=(MICRO, width // 384),
-            in_specs=[pair_block(384)] + [TABLE] * 3,
-            out_specs=[pair_block(128), pair_block(384)],
-        ),
-        cost_estimate=FREE,
-    )(lengths, qkv, *tables)
-
-
-def multiply(a, w, transposed, tile, dtype):
-    height, depth = a.shape
-    width = w.shape[0] if transposed else w.shape[1]
-
-    def kernel(a_ref, w_ref, o_ref):
-        form = mm_nt if transposed else mm
-        o_ref[...] = form(a_ref[...], w_ref[...]).astype(dtype)
-
-    if transposed:
-        w_spec = pl.BlockSpec((tile, depth), lambda j: (j, 0))
-    else:
-        w_spec = pl.BlockSpec((depth, tile), lambda j: (0, j))
-    return pl.pallas_call(
-        kernel,
-        out_shape=jax.ShapeDtypeStruct((height, width), dtype),
-        grid=(width // tile,),
-        in_specs=[whole(a.shape), w_spec],
-        out_specs=pl.BlockSpec((height, tile), lambda j: (0, j)),
-        cost_estimate=FREE,
-    )(a, w)
-
-
-def split_product(parts, w, transposed, tile, cost=FREE):
-    count = len(parts)
-    height = parts[0].shape[0]
-    width = w.shape[0] if transposed else w.shape[1]
-    steps = width // tile
-    half = steps // 2
-
-    def kernel(*refs):
-        form = mm_nt if transposed else mm
-        total = form(refs[0][...], refs[count][...])
-        for at in range(1, count):
-            total = total + form(refs[at][...], refs[count + at][...])
-        kept_ref, sent_ref = refs[2 * count :]
-        step = pl.program_id(0)
-
-        @pl.when(step < half)
-        def _():
-            sent_ref[...] = total.astype(BF16)
-
-        @pl.when(step >= half)
-        def _():
-            kept_ref[...] = total
-
-    def w_spec(at, depth):
-        if transposed:
-            return pl.BlockSpec((tile, depth), lambda j: (lax.rem(j + half, steps), at))
-        return pl.BlockSpec((depth, tile), lambda j: (at, lax.rem(j + half, steps)))
-
-    return pl.pallas_call(
-        kernel,
-        out_shape=(
-            jax.ShapeDtypeStruct((height, width // 2), F32),
-            jax.ShapeDtypeStruct((height, width // 2), BF16),
-        ),
-        grid=(steps,),
-        in_specs=[whole(part.shape) for part in parts]
-        + [w_spec(at, part.shape[1]) for at, part in enumerate(parts)],
-        out_specs=(
-            pl.BlockSpec((height, tile), lambda j: (0, jnp.maximum(j - half, 0))),
-            pl.BlockSpec((height, tile), lambda j: (0, jnp.minimum(j, half - 1))),
-        ),
-        cost_estimate=cost,
-    )(*parts, *([w] * count))
-
-
 def feed_kernel(x_ref, gate_ref, up_ref, da_ref, hidden_ref, dg_ref, du_ref):
     x = x_ref[...]
     gate = mm(x, gate_ref[...])
@@ -253,78 +149,6 @@
     )(x, pair_w, pair_w, hidden_grad)
 
 
-def swap_kernel(plan, given, count, *refs):
-    weights, outs = refs[:given], refs[given : given + count]
-    rest = refs[given + count :]
-    held, (send_sem, recv_sem, in_sem, out_sem) = rest[: len(plan)], rest[len(plan) :]
-    row = lax.axis_index("row")
-    barrier = pltpu.get_barrier_semaphore()
-    pl.semaphore_signal(
-        barrier, inc=1, device_id={"row": 1 - row}, device_id_type=pl.DeviceIdType.MESH
-    )
-    remote, local = [], []
-    for at, (source, by_rows, out, start, offset, size) in enumerate(plan):
-        weight = weights[source]
-        height, width = weight.shape
-
-        def part(index):
-            if by_rows:
-                return weight.at[pl.ds(pl.multiple_of(index * size, size), size), :]
-            first = pl.multiple_of(index * (width // 2) + start, 128)
-            return weight.at[:, pl.ds(first, size)]
-
-        def place(second):
-            if by_rows:
-                return outs[out].at[:, pl.ds(second * width, width)]
-            return outs[out].at[pl.ds(second * height, height), pl.ds(offset, size)]
-
-        remote.append(
-            pltpu.make_async_remote_copy(
-                src_ref=part(1 - row),
-                dst_ref=place(1),
-                send_sem=send_sem.at[at],
-                recv_sem=recv_sem.at[at],
-                device_id={"row": 1 - row},
-                device_id_type=pl.DeviceIdType.MESH,
-            )
-        )
-        local.append(
-            (
-                pltpu.make_async_copy(part(row), held[at], in_sem.at[at]),
-                pltpu.make_async_copy(held[at], place(0), out_sem.at[at]),
-            )
-        )
-    for fetch, _ in local:
-        fetch.start()
-    pl.semaphore_wait(barrier, 1)
-    for copy in remote:
-        copy.start()
-    for fetch, store in local:
-        fetch.wait()
-        store.start()
-    for _, store in local:
-        store.wait()
-    for copy in remote:
-        copy.wait()
-
-
-def swap_weights(weights, plan, shapes, identity):
-    held = []
-    for source, by_rows, _, _, _, size in plan:
-        height, width = weights[source].shape
-        held.append((size, width) if by_rows else (height, size))
-    sems = pltpu.SemaphoreType.DMA((len(plan),))
-    return pl.pallas_call(
-        lambda *refs: swap_kernel(plan, len(weights), len(shapes), *refs),
-        out_shape=[jax.ShapeDtypeStruct(shape, BF16) for shape in shapes],
-        in_specs=[pl.BlockSpec(memory_space=pl.ANY)] * len(weights),
-        out_specs=[pl.BlockSpec(memory_space=pl.ANY)] * len(shapes),
-        scratch_shapes=[pltpu.VMEM(shape, BF16) for shape in held] + [sems] * 4,
-        compiler_params=pltpu.CompilerParams(collective_id=identity, has_side_effects=True),
-        cost_estimate=FREE,
-    )(*weights)
-
-
 MESH = pl.DeviceIdType.MESH
 
 
@@ -450,12 +274,10 @@
     dqkv,
     dqkv_row,
     first_mine,
-    first_came,
+    first_theirs,
     branch,
     mixed_mine,
-    mixed_came,
-    mixed_row,
-    mixed_came_row,
+    mixed_theirs,
     both,
     pieces,
     gate_out,
@@ -478,6 +300,10 @@
     dqkv_came,
     dqkv_came_row,
     branch_came,
+    first_came,
+    mixed_came,
+    mixed_row,
+    mixed_came_row,
     turned_left,
     gate_stage,
     up_stage,
@@ -516,6 +342,10 @@
     dqkv_x = swap(dqkv, dqkv_came, 2, {"dp": partner})
     up_across = swap(up_came, up_came_row, 3, {"row": 1 - row})
     dqkv_across = swap(dqkv_came, dqkv_came_row, 4, {"row": 1 - row})
+    first_x = swap(first_theirs, first_came, 5, {"dp": partner})
+    mixed_x = swap(mixed_theirs, mixed_came, 6, {"dp": partner})
+    mixed_r = swap(mixed_mine, mixed_row, 7, {"row": 1 - row})
+    mixed_across = swap(mixed_came, mixed_came_row, 8, {"row": 1 - row})
 
     stores = []
 
@@ -583,8 +413,11 @@
     gain_copy(0).start()
     gate_line.run(0, 1)
     up_x.start()
+    mixed_x.start()
     branch_x.start()
+    first_x.start()
     dqkv_x.start()
+    mixed_r.start()
 
     def send_back(step, _):
         returned(step).start()
@@ -618,8 +451,8 @@
     gate_line.finish()
     store_wide(gate_line)
 
-    turned_left[:, :depth] = first_mine[...].T
-    turned_left[:, depth:] = first_came[...].T
+    mixed_x.wait_recv()
+    mixed_across.start()
     branch_x.wait_recv()
 
     def side(start, mine, came):
@@ -630,10 +463,15 @@
         tiles_loop(branch.shape[1], 512, body)
 
     side(0, mixed_mine, mixed_came)
+    mixed_r.wait_recv()
+    mixed_across.wait_recv()
     side(mixed_mine.shape[1], mixed_row, mixed_came_row)
     output_line.run(0, 1)
     up_line.run(1, 2)
     gain_step(1)
+    first_x.wait_recv()
+    turned_left[:, :depth] = first_mine[...].T
+    turned_left[:, depth:] = first_came[...].T
     dqkv_x.wait_recv()
     dqkv_across.start()
     wide(qkv_grads, 0, dqkv, dqkv_came)
@@ -661,7 +499,8 @@
     lax.fori_loop(1, groups, get_back, 0)
     for step in range(gain_steps):
         gain_copy(step).wait_send()
-    for copy in (up_x, branch_x, dqkv_x, up_across, dqkv_across):
+    copies = (up_x, branch_x, dqkv_x, up_across, dqkv_across)
+    for copy in copies + (first_x, mixed_x, mixed_r, mixed_across):
         copy.wait_send()
     for copy in stores:
         copy.wait()
@@ -699,6 +538,404 @@
         return 0
 
     lax.fori_loop(0, ROWS // size, one, 0)
+
+
+def deal_kernel(order_ref, tokens_ref, dealt_ref):
+    groups = tokens_ref.shape[1]
+
+    def one(at, _):
+        micro, slot = at // groups, lax.rem(at, groups)
+        dealt_ref[micro, slot] = tokens_ref[micro, order_ref[micro, slot]]
+        return 0
+
+    lax.fori_loop(0, MICRO * groups, one, 0)
+
+
+def deal(order, tokens):
+    vmem = pl.BlockSpec(memory_space=pltpu.VMEM)
+    return pl.pallas_call(
+        deal_kernel,
+        out_shape=jax.ShapeDtypeStruct(tokens.shape, BF16),
+        in_specs=[pl.BlockSpec(memory_space=pltpu.SMEM), vmem],
+        out_specs=vmem,
+        cost_estimate=FREE,
+    )(order, tokens)
+
+
+def front_kernel(
+    dealt,
+    top_block,
+    gain_first,
+    gain_second,
+    key_live,
+    cos,
+    first,
+    second,
+    query_weight,
+    key_weight,
+    value_weight,
+    output_weight,
+    gate_weight,
+    up_weight,
+    down_weight,
+    pair_out,
+    down_out,
+    qkv_out,
+    out_out,
+    x_in,
+    top_half,
+    top_came,
+    normed_first,
+    turned,
+    mixed,
+    middle,
+    inverse_first,
+    inverse_second,
+    normed_second,
+    hidden_grad,
+    qkv_w,
+    out_w,
+    pair_held,
+    down_held,
+    tiles,
+    x_came,
+    x_half,
+    x_other,
+    top_col,
+    top_row,
+    sent,
+    row_came,
+    kept,
+    summed,
+    col_came,
+    low,
+    low_came,
+    deal_sems,
+    weight_sems,
+    local_sems,
+    swap_sems,
+    tile_sems,
+):
+    groups = dealt.shape[1]
+    dp, row, col = lax.axis_index("dp"), lax.axis_index("row"), lax.axis_index("col")
+    partner = {"dp": dp + 1 - 2 * lax.rem(dp, 2)}
+    across = {"row": 1 - row}
+    beside = {"col": 1 - col}
+    half, block = D // 2, D // 4
+    heads = query_weight.shape[1] // 2
+    quarter = gate_weight.shape[1] // 2
+    pending = []
+
+    def remote(source, target, sems, at, device):
+        copy = pltpu.make_async_remote_copy(
+            src_ref=source,
+            dst_ref=target,
+            send_sem=sems.at[0, at],
+            recv_sem=sems.at[1, at],
+            device_id=device,
+            device_id_type=MESH,
+        )
+        copy.start()
+        pending.append(copy)
+        return copy
+
+    def swap(source, target, at, device):
+        return remote(source, target, swap_sems, at, device)
+
+    def columns(w, index, start, size):
+        begin = pl.multiple_of(index * (w.shape[1] // 2) + start, 128)
+        return w.at[:, pl.ds(begin, size)]
+
+    def rows_half(w, index):
+        size = w.shape[0] // 2
+        return w.at[pl.ds(pl.multiple_of(index * size, size), size), :]
+
+    locals_started = []
+
+    def local(source, target):
+        copy = pltpu.make_async_copy(source, target, local_sems.at[len(locals_started)])
+        copy.start()
+        locals_started.append(copy)
+        return copy
+
+    own_now = []
+    for kind, w in enumerate((query_weight, key_weight, value_weight)):
+        for at in range(0, heads, 128):
+            there = pl.ds(3 * at + 128 * kind, 128)
+            own_now.append(local(columns(w, row, at, 128), qkv_w.at[pl.ds(0, half), there]))
+    own_now.append(local(rows_half(output_weight, row), out_w.at[:, pl.ds(0, half)]))
+    own_gate = local(columns(gate_weight, row, 0, quarter), pair_held.at[0])
+    own_up = local(columns(up_weight, row, 0, quarter), pair_held.at[1])
+    own_down = local(rows_half(down_weight, row), down_held)
+    own_rows = local(dealt.at[:, dp], x_in.at[:, dp])
+    others = [(jnp.int32(1), {"dp": lax.rem(dp + step, groups)}) for step in range(1, groups)]
+    greet(*others, (jnp.int32(1), across), (jnp.int32(1), beside))
+
+    def dealing(step, micro):
+        target = lax.rem(dp + step, groups)
+        return pltpu.make_async_remote_copy(
+            src_ref=dealt.at[micro, target],
+            dst_ref=x_in.at[micro, dp],
+            send_sem=deal_sems.at[0, micro, step],
+            recv_sem=deal_sems.at[1, micro, step],
+            device_id={"dp": target},
+            device_id_type=MESH,
+        )
+
+    for micro in range(MICRO):
+
+        def send_rows(step, _):
+            dealing(step, micro).start()
+            return 0
+
+        lax.fori_loop(1, groups, send_rows, 0)
+    top_c = swap(top_block, top_col, 0, beside)
+    weights_now = []
+    for kind, w in enumerate((query_weight, key_weight, value_weight)):
+        for at in range(0, heads, 128):
+            there = qkv_w.at[pl.ds(half, half), pl.ds(3 * at + 128 * kind, 128)]
+            weights_now.append(
+                remote(columns(w, 1 - row, at, 128), there, weight_sems, len(weights_now), across)
+            )
+    weights_now.append(
+        remote(
+            rows_half(output_weight, 1 - row),
+            out_w.at[:, pl.ds(half, half)],
+            weight_sems,
+            len(weights_now),
+            across,
+        )
+    )
+    weights_late = []
+    for k, w in enumerate((gate_weight, up_weight)):
+        there = pair_out.at[pl.ds(half, half), pl.ds(k * quarter, quarter)]
+        weights_late.append(
+            remote(
+                columns(w, 1 - row, 0, quarter), there, weight_sems, len(weights_now) + k, across
+            )
+        )
+    own_gate.wait()
+    own_up.wait()
+    store_gate = local(pair_held.at[0], pair_out.at[pl.ds(0, half), pl.ds(0, quarter)])
+    store_up = local(pair_held.at[1], pair_out.at[pl.ds(0, half), pl.ds(quarter, quarter)])
+    own_down.wait()
+    store_down = local(down_held, down_out.at[:, pl.ds(0, half)])
+
+    def half_of(own, came):
+        return jnp.where(
+            col == 0,
+            jnp.concatenate([own, came], axis=1),
+            jnp.concatenate([came, own], axis=1),
+        )
+
+    own_rows.wait()
+    x_c = []
+    for micro in range(MICRO):
+
+        def take_rows(step, _):
+            dealing(step, micro).wait_recv()
+            return 0
+
+        lax.fori_loop(1, groups, take_rows, 0)
+        x_c.append(swap(x_in.at[micro], x_came.at[micro], 1 + micro, beside))
+    top_c.wait_recv()
+
+    def top_rows(rows):
+        top_half[rows, :] = half_of(top_block[rows, :], top_col[rows, :])
+
+    rows_loop(top_rows)
+    top_x = swap(top_half, top_came, 3, partner)
+
+    def micro_rows(micro):
+        return pl.ds(micro * SL, SL)
+
+    x_r = []
+    for micro in range(MICRO):
+        x_c[micro].wait_recv()
+        own = x_in[micro].reshape(SL, block)
+        came = x_came[micro].reshape(SL, block)
+        x_half[micro_rows(micro), :] = half_of(own, came)
+        rows = micro_rows(micro)
+        x_r.append(swap(x_half.at[rows, :], x_other.at[rows, :], 4 + micro, across))
+        if micro == 0:
+            for copy in own_now:
+                copy.wait()
+            for copy in weights_now:
+                copy.wait_recv()
+    top_r = swap(top_half, top_row, 6, across)
+    down_there = down_out.at[:, pl.ds(half, half)]
+    down_r = remote(
+        rows_half(down_weight, 1 - row), down_there, weight_sems, len(weights_now) + 2, across
+    )
+    store_qkv = local(qkv_w, qkv_out)
+    store_out = local(out_w, out_out)
+
+    lower = lax.broadcasted_iota(jnp.int32, (SL, SL), 1) <= lax.broadcasted_iota(
+        jnp.int32, (SL, SL), 0
+    )
+
+    def norm_rows(own_ref, other_ref, gain, inverse_ref, out_ref, micro):
+        def body(j, _):
+            rows = pl.ds(pl.multiple_of(micro * SL + j * 64, 64), 64)
+            own = own_ref[rows, :].astype(F32)
+            other = other_ref[rows, :].astype(F32)
+            total = jnp.sum(own * own, axis=1, keepdims=True)
+            total = total + jnp.sum(other * other, axis=1, keepdims=True)
+            inverse = lax.rsqrt(total / D + EPSILON)
+            inverse_ref[rows, :] = inverse
+            out_ref[rows, :half] = (own * inverse * gain[:, :half]).astype(BF16)
+            out_ref[rows, half:] = (other * inverse * gain[:, half:]).astype(BF16)
+            return 0
+
+        lax.fori_loop(0, SL // 64, body, 0)
+
+    sum_c = []
+    for micro in range(MICRO):
+        rows = micro_rows(micro)
+        x_r[micro].wait_recv()
+        norm_rows(x_half, x_other, gain_first, inverse_first, normed_first, micro)
+        allowed = lower & (key_live[micro : micro + 1, :] > 0.5)
+
+        def attend(at, _):
+            there = pl.multiple_of(at * 768, 128)
+            qkv = mm(normed_first[rows, :], qkv_w[:, pl.ds(there, 768)])
+            for pair in range(2):
+                qr, kr, vr, out = head_outputs(
+                    qkv[:, pair * 384 : pair * 384 + 384], allowed, cos[...], first[...], second[...]
+                )
+                begin = there + pair * 384
+                for kind, value in enumerate((qr, kr, vr)):
+                    turned[rows, pl.ds(pl.multiple_of(begin + kind * 128, 128), 128)] = value
+                mixed[rows, pl.ds(pl.multiple_of(at * 256 + pair * 128, 128), 128)] = out
+            return 0
+
+        lax.fori_loop(0, heads // 256, attend, 0)
+        sent[rows, :] = mm(mixed[rows, :], out_w[:, half:]).astype(BF16)
+        sum_r = swap(sent.at[rows, :], row_came.at[rows, :], 7 + micro, across)
+        kept[...] = mm(mixed[rows, :], out_w[:, :half])
+        sum_r.wait_recv()
+        summed[rows, :] = (kept[...] + row_came[rows, :].astype(F32)).astype(BF16)
+        sum_c.append(swap(summed.at[rows, :], col_came.at[rows, :], 9 + micro, beside))
+
+    top_r.wait_recv()
+    store_down.wait()
+    down_r.wait_recv()
+
+    def da_body(j, slot):
+        total = mm_nt(top_half[...], tiles[slot, :, :half])
+        total = total + mm_nt(top_row[...], tiles[slot, :, half:])
+        hidden_grad[:, pl.ds(pl.multiple_of(j * 256, 256), 256)] = total
+
+    stream(
+        lambda j: [down_out.at[pl.ds(pl.multiple_of(j * 256, 256), 256), :]],
+        lambda slot: [tiles.at[slot]],
+        tile_sems,
+        quarter // 256,
+        da_body,
+    )
+
+    low_r = []
+    for micro in range(MICRO):
+        rows = micro_rows(micro)
+        sum_c[micro].wait_recv()
+
+        def middle_rows(j, _):
+            here = pl.ds(pl.multiple_of(micro * SL + j * 64, 64), 64)
+            total = x_half[here, :].astype(F32) + (
+                summed[here, :].astype(F32) + col_came[here, :].astype(F32)
+            )
+            middle[here, :] = total
+            low[here, :] = total.astype(BF16)
+            return 0
+
+        lax.fori_loop(0, SL // 64, middle_rows, 0)
+        low_r.append(swap(low.at[rows, :], low_came.at[rows, :], 11 + micro, across))
+        low_r[micro].wait_recv()
+        norm_rows(low, low_came, gain_second, inverse_second, normed_second, micro)
+
+    top_x.wait_recv()
+    for copy in weights_late:
+        copy.wait_recv()
+    for copy in pending:
+        copy.wait_send()
+
+    def close(step, _):
+        for micro in range(MICRO):
+            dealing(step, micro).wait_send()
+        return 0
+
+    lax.fori_loop(1, groups, close, 0)
+    for copy in (store_gate, store_up, store_qkv, store_out):
+        copy.wait()
+
+
+def front(line, identity, *values):
+    dealt, query_weight, gate_weight = values[0], values[8], values[12]
+    groups = dealt.shape[1]
+    half, block = D // 2, D // 4
+    heads = query_weight.shape[1] // 2
+    quarter = gate_weight.shape[1] // 2
+    vmem = pl.BlockSpec(memory_space=pltpu.VMEM)
+    anywhere = pl.BlockSpec(memory_space=pl.ANY)
+
+    def array(*shape, dtype=BF16):
+        return jax.ShapeDtypeStruct(shape, dtype)
+
+    def buffer(*shape, dtype=BF16):
+        return pltpu.VMEM(shape, dtype)
+
+    sem = pltpu.SemaphoreType.DMA
+    now = 3 * (heads // 128) + 1
+    return pl.pallas_call(
+        front_kernel,
+        out_shape=[
+            array(D, 2 * quarter),
+            array(quarter, D),
+            array(D, 3 * heads),
+            array(heads, D),
+            array(*dealt.shape),
+            array(ROWS, half),
+            array(ROWS, half),
+            array(ROWS, D),
+            array(ROWS, 3 * heads),
+            array(ROWS, heads),
+            array(ROWS, half, dtype=F32),
+            array(ROWS, 1, dtype=F32),
+            array(ROWS, 1, dtype=F32),
+            array(ROWS, D),
+            array(ROWS, quarter, dtype=F32),
+        ],
+        in_specs=[vmem] * 8 + [anywhere] * 7,
+        out_specs=[anywhere] * 4 + [vmem] * 11,
+        scratch_shapes=[
+            buffer(D, 3 * heads),
+            buffer(heads, D),
+            buffer(2, half, quarter),
+            buffer(quarter, half),
+            buffer(2, 256, D),
+            buffer(*dealt.shape),
+            buffer(ROWS, half),
+            buffer(ROWS, half),
+            buffer(ROWS, block),
+            buffer(ROWS, half),
+            buffer(ROWS, half),
+            buffer(ROWS, half),
+            buffer(SL, half, dtype=F32),
+            buffer(ROWS, half),
+            buffer(ROWS, half),
+            buffer(ROWS, half),
+            buffer(ROWS, half),
+            sem((2, MICRO, groups)),
+            sem((2, now + 3)),
+            sem((now + 9,)),
+            sem((2, 13)),
+            sem((2, 2)),
+        ],
+        compiler_params=pltpu.CompilerParams(
+            collective_id=identity, has_side_effects=True, vmem_limit_bytes=67043328
+        ),
+        cost_estimate=FREE,
+    )(*values)
 
 
 def chain_kernel(
@@ -710,7 +947,6 @@
     second_theirs,
     top_half,
     top_came,
-    mixed_came,
     pair_w,
     down_w,
     qkv_w,
@@ -733,7 +969,6 @@
     dqkv,
     dqkv_row,
     branch,
-    mixed_came_row,
     both_out,
     pieces_out,
     gate_row,
@@ -855,7 +1090,6 @@
     pair_c = begin(swap(summed, col_came, 3, beside))
     gate_r = begin(swap(gate_grad, gate_row, 4, across))
     up_r = begin(swap(up_grad, up_row, 5, across))
-    mixed_r = begin(swap(mixed_came, mixed_came_row, 6, across))
 
     def down_product(start, target, dtype):
         def body(j, slot):
@@ -1103,7 +1337,7 @@
     down_line.finish()
     down_store = pltpu.make_async_copy(down_line.stage, down_out, copy_sems.at[1])
     down_store.start()
-    for copy in (up_r, mixed_r, dqkv_r):
+    for copy in (up_r, dqkv_r):
         copy.wait_recv()
     for copy in pending:
         copy.wait_send()
@@ -1114,13 +1348,12 @@
     hidden, gate_grad = values[:2]
     quarter = hidden.shape[1]
     narrow = values[3].shape[1]
-    mixed_width = values[7].shape[1]
-    qkv_width = values[12].shape[1]
+    qkv_width = values[11].shape[1]
     half, block = D // 2, D // 4
     rows = quarter // 2
     vmem = pl.BlockSpec(memory_space=pltpu.VMEM)
     anywhere = pl.BlockSpec(memory_space=pl.ANY)
-    outside = {8, 9, 10, 11, 13}
+    outside = {7, 8, 9, 10, 12}
 
     def array(*shape, dtype=BF16):
         return jax.ShapeDtypeStruct(shape, dtype)
@@ -1136,7 +1369,6 @@
         (array(ROWS, qkv_width), vmem),
         (array(ROWS, qkv_width), anywhere),
         (array(ROWS, half), vmem),
-        (array(ROWS, mixed_width), anywhere),
         (array(2 * ROWS, block), vmem),
         (array(2, block, dtype=F32), vmem),
         (array(ROWS, quarter), anywhere),
@@ -1198,7 +1430,7 @@
     sizes = [(h // line, w) for h, w in zip(heights, widths)]
     vmem = pl.BlockSpec(memory_space=pltpu.VMEM)
     anywhere = pl.BlockSpec(memory_space=pl.ANY)
-    both, gains = values[14:]
+    both, gains = values[12:]
     height = sizes[0][0]
     gain_steps = both.shape[1].bit_length() - 1
 
@@ -1220,17 +1452,18 @@
             jax.ShapeDtypeStruct(both.shape, BF16),
             array(*gains.shape),
         ],
-        in_specs=[vmem] * 14 + [anywhere, vmem],
+        in_specs=[vmem] * 12 + [anywhere, vmem],
         out_specs=[anywhere] * 7 + [vmem],
         scratch_shapes=[buffer(2, line - 1, *size) for size in sizes]
         + [buffer(h, w) for h, w in zip(heights[1:], widths[1:])]
         + [buffer(*up.shape)] * 2
         + [buffer(*dqkv.shape)] * 2
-        + [buffer(*branch.shape)]
+        + [buffer(*branch.shape), buffer(*values[7].shape)]
+        + [buffer(*values[10].shape)] * 3
         + [buffer(rows, 2 * tokens)]
         + [pltpu.VMEM(size, F32) for size in sizes]
         + [pltpu.SemaphoreType.DMA((2, 2, line - 1, count)) for count in pieces]
-        + [pltpu.SemaphoreType.DMA((2, 5)), pltpu.SemaphoreType.DMA((6 + widths[2] // 128,))]
+        + [pltpu.SemaphoreType.DMA((2, 9)), pltpu.SemaphoreType.DMA((6 + widths[2] // 128,))]
         + [pltpu.VMEM((2, gain_steps, *gains.shape), F32)]
         + [
             pltpu.SemaphoreType.DMA((2, both.shape[1])),
@@ -1298,9 +1531,6 @@
     def over_col(v):
         return lax.ppermute(v, "col", SWAP)
 
-    def over_x(v):
-        return lax.ppermute(v, "dp", [(i, i ^ 1) for i in range(groups)])
-
     def ordered(own, other, index, axis=-1):
         return jnp.where(
             index == 0,
@@ -1327,110 +1557,58 @@
         token[:] = [value]
         return value
 
-    def arrive(*values):
-        out = ordered_after(*values)
-        mark(out[0] if len(values) > 1 else out)
-        return out
-
-    gathered = jnp.take_along_axis(tokens, deal_order[:, :, None, None], axis=1)
-    gathered = mark(lax.optimization_barrier(gathered))
-    dealt = lax.all_to_all(gathered, "dp", split_axis=1, concat_axis=2, tiled=True)
     own_order = lax.dynamic_slice_in_dim(deal_order, dp, 1, 1)
     own_lengths = jnp.take_along_axis(lengths, own_order, axis=1)[:, 0]
     tables = rope_tables()
     live = (jnp.arange(SL, dtype=jnp.int32)[None, :] < own_lengths[:, None]).reshape(ROWS, 1)
     key_live = live.reshape(MICRO, SL).astype(F32)
     top_block = jnp.where(live, cotangent.reshape(ROWS, block), 0.0).astype(BF16)
-
     gains = jnp.stack([attention_gain, feed_gain])
     gains_half = ordered(gains, over_col(gains), col)
-    gains_other = over_row(gains_half)
-    gains_full = jnp.concatenate([gains_half, gains_other], axis=1)
-
-    top_col = over_col(top_block)
-    quarter = gate_weight.shape[1] // 2
-    gate_weight, up_weight = ordered_after(gate_weight, up_weight)
-    (pair_w,) = swap_weights(
-        (gate_weight, up_weight),
-        ((0, False, 0, 0, 0, quarter), (1, False, 0, 0, quarter, quarter)),
-        ((D, 2 * quarter),),
+    gains_full = jnp.concatenate([gains_half, over_row(gains_half)], axis=1)
+    (
+        pair_w,
+        down_w,
+        qkv_w,
+        out_w,
+        x_block,
+        top_half,
+        top_came,
+        normed_first,
+        turned,
+        mixed,
+        middle,
+        inverse_first,
+        inverse_second,
+        normed_second,
+        hidden_grad,
+    ) = front(
+        line,
         0,
+        deal(deal_order, tokens),
+        top_block,
+        gains_full[:1],
+        gains_full[1:],
+        key_live,
+        *tables,
+        query_weight,
+        key_weight,
+        value_weight,
+        output_weight,
+        gate_weight,
+        up_weight,
+        down_weight,
     )
-    mark(pair_w)
-    x_block = arrive(dealt).reshape(ROWS, block)
-    x_came = over_col(x_block)
-    heads = query_weight.shape[1] // 2
-    query_weight, key_weight, value_weight, output_weight = ordered_after(
-        query_weight, key_weight, value_weight, output_weight
-    )
-    plan = [
-        (kind, False, 0, at, 3 * at + 128 * kind, 128)
-        for kind in range(3)
-        for at in range(0, heads, 128)
-    ]
-    qkv_w, out_w = swap_weights(
-        (query_weight, key_weight, value_weight, output_weight),
-        tuple(plan) + ((3, True, 1, 0, 0, heads),),
-        ((D, 3 * heads), (heads, D)),
-        1,
-    )
-    mark(qkv_w)
-    top_half = ordered(top_block, arrive(top_col), col)
-    top_half = mark(lax.optimization_barrier(top_half))
-    x_half = ordered(x_block, arrive(x_came), col)
-    x_half = mark(lax.optimization_barrier(x_half))
-    top_came = over_x(top_half)
-    top_row = over_row(top_half)
-
-    x_other = arrive(over_row(x_half))
-    x_full = jnp.concatenate([x_half, x_other], axis=1).astype(F32)
-    inverse_first = lax.rsqrt(jnp.mean(x_full * x_full, axis=1, keepdims=True) + EPSILON)
-    normed_first = (x_full * inverse_first * gains_full[0][None, :]).astype(BF16)
-    normed_first = mark(lax.optimization_barrier(normed_first))
-    qkv = multiply(normed_first, qkv_w, False, 384, F32)
-    mixed, turned = attend_forward(own_lengths, qkv, tables)
-    kept, sent = split_product([mixed], out_w, False, 512)
-    mark(sent)
-    came = arrive(over_row(sent))
-    summed = (kept + came.astype(F32)).astype(BF16)
-    summed = mark(lax.optimization_barrier(summed))
-    summed_other = over_col(summed)
-    top_row = arrive(top_row)
+    x_block = x_block.reshape(ROWS, block)
     narrow = half // groups
-    first_mine, first_theirs = x_parts(normed_first[:, :half], narrow)
-    top_full = jnp.concatenate([top_half, top_row], axis=1)
-    (down_w,) = swap_weights(
-        (ordered_after(down_weight),),
-        ((0, True, 0, 0, 0, down_weight.shape[0] // 2),),
-        ((down_weight.shape[0] // 2, D),),
-        2,
-    )
-    hidden_grad = mark(multiply(top_full, down_w, True, 512, F32))
-    top_came = arrive(top_came)
-    mixed_mine, mixed_theirs = x_parts(mixed, 2 * mixed.shape[1] // groups)
-    first_came = over_x(ordered_after(first_theirs))
-    mixed_came = over_x(ordered_after(mixed_theirs))
-    mixed_row = over_row(mixed_mine)
-    summed_other = arrive(summed_other)
-    middle = x_half.astype(F32) + (summed.astype(F32) + summed_other.astype(F32))
-
-    middle_low = middle.astype(BF16)
-    middle_low, middle = lax.optimization_barrier((middle_low, middle))
-    mark(middle_low)
-    middle_other = arrive(over_row(middle_low))
-    middle_full = jnp.concatenate([middle_low, middle_other], axis=1).astype(F32)
-    inverse_second = lax.rsqrt(
-        jnp.mean(middle_full * middle_full, axis=1, keepdims=True) + EPSILON
-    )
-    normed_second = (middle_full * inverse_second * gains_full[1][None, :]).astype(BF16)
-    normed_second = mark(lax.optimization_barrier(normed_second))
     hidden, gate_grad, up_grad = feed_forward(normed_second, pair_w, hidden_grad)
     mark(hidden)
-    first_came, mixed_came, mixed_row = arrive(first_came, mixed_came, mixed_row)
 
     def own_block(v):
         return lax.dynamic_slice_in_dim(v, col * block, block, 1)
 
+    first_mine, first_theirs = x_parts(normed_first[:, :half], narrow)
+    mixed_mine, mixed_theirs = x_parts(mixed, 2 * mixed.shape[1] // groups)
     second_mine, second_theirs = x_parts(normed_second[:, :half], narrow)
     (
         down_sum,
@@ -1440,7 +1618,6 @@
         dqkv,
         dqkv_row,
         branch,
-        mixed_came_row,
         both,
         pieces,
         _,
@@ -1457,7 +1634,6 @@
             second_theirs,
             top_half,
             top_came,
-            mixed_came,
             pair_w,
             down_w,
             qkv_w,
@@ -1487,12 +1663,10 @@
             dqkv,
             dqkv_row,
             first_mine,
-            first_came,
+            first_theirs,
             branch,
             mixed_mine,
-            mixed_came,
-            mixed_row,
-            mixed_came_row,
+            mixed_theirs,
             both.reshape(2 * MICRO, groups, SL // groups, block),
             pieces,
         ),

time: 501 us -> 472 us (0.942)
  other arithmetic: 25.5 us -> 11.8 us
  waiting for transfers between devices: 12.8 us -> 0.01 us
  starting transfers between devices: 15.8 us -> 3.09 us
  Pallas kernels: 425 us -> 437 us
    pallas_call x7 -> x2, Pallas kernels: 61.2 us -> 76.1 us  [the longest x1 74 us: front(): pl.pallas_call(front_kernel, out_shape=[array(D, 2 * quarter), array(quar...]
    ppermute x4 -> x1, waiting for transfers between devices: 11 us -> 0.01 us  [over_col(): return lax.ppermute(v, 'col', SWAP)]
    convert_element_type x4 -> x0, other arithmetic: 10.2 us -> none  [the longest x1 3.22 us: per_device(): middle_low = middle.astype(BF16)]
    all_to_all x1 -> x0, starting transfers between devices: 7.25 us -> none  [per_device(): lax.all_to_all(gathered, 'dp', split_axis=1, concat_axis=2, tiled=True)]
    unnamed x42 -> x24, local copies, waits for them, and re-layouts: 10.5 us -> 10.5 us
  transfers between devices with their start and end apart: 14 -> 2, of which waited for: 6 -> 0; matrix products, arithmetic and copies ran while one was open for 4% -> 2% of each run, Pallas kernels for 11% -> 0%
where the time goes in v1:
time: 472 us; the launch traced here: 470 us
  Pallas kernels  437 us (93%)
  local copies, waits for them, and re-layouts  17.4 us (4%)
  other arithmetic  11.8 us (2%)
    pallas_call x1, Pallas kernels, tail_sums(): pl.pallas_call(lambda *refs: tail_kernel(line, *refs), out_shape=[array(*...  230 us
    pallas_call x1, Pallas kernels, chain(): pl.pallas_call(lambda *refs: chain_kernel(line, *refs), out_shape=[shape...  112 us
    pallas_call x1, Pallas kernels, front(): pl.pallas_call(front_kernel, out_shape=[array(D, 2 * quarter), array(quar...  74 us
    pallas_call x1, Pallas kernels, feed_forward(): pl.pallas_call(feed_kernel, out_shape=(jax.ShapeDtypeStruct((height, widt...  17.1 us
    unnamed x24, local copies, waits for them, and re-layouts  10.5 us
  transfers between devices with their start and end apart: 2, of which 0 were waited for; matrix products, arithmetic and copies ran while one was open for 2% of the time, Pallas kernels for 0%

profile of v1, /device:TPU:0, one launch (start us, length us, event | category | flops | bytes accessed | tf_op | source)
XLA Modules:
  0.0 470.5 jit_solution(10002145651014077747)
XLA Ops:
  1.4 3.0 collective-permute-start
  4.4 0.9 fusion.4
  5.6 1.3 gather_fusion
  7.0 0.9 fusion.3
  9.1 1.0 pad_maximum_fusion.8
  10.1 2.0 bitcast_select_fusion.top_block
  12.1 0.8 pad_maximum_fusion.6.cos.refs_19_
  12.9 2.1 shard_map.212.dealt
  16.9 74.0 %shard_map.213 = (bf16[2048,4096]{1,0:T(8,128)(2,1)}, bf16[2048,2048]{1,0:T(8,128)(2,1)}, bf16[2048,1536]{1,0:T(8,128)(2,1)}, bf16[512,2048]{1,0:T(8,128)(2,1)},...) custom-call(bf16[2,8,32,512]{3,2,1,0:T(8,128)(2,1)} %shard_map.212.d, ...), custom_call_target="tpu_custom_call" | custom-call | tf_op jit(solution)/shard_map/pallas_call | solution.py:889
  90.9 1.1 fusion.8
  92.1 1.8 fusion.6
  93.9 17.1 %shard_map.214 = (bf16[512,2048]{1,0:T(8,128)(2,1)}, bf16[512,2048]{1,0:T(8,128)(2,1)}, bf16[512,2048]{1,0:T(8,128)(2,1)}) custom-call(bf16[512,2048]{1,0:T(8,128)(2,1)} %get-tuple-element.84.x_ref, bf16[2048,4096]{1,0:T(8,128)(2,1)} %get-tuple-element.107.gate_ref.up_ref.refs_7_, bf16[2048,4096]{1,0:T(8,128)(2,1)} %get-tuple-element.107.gate_ref.up_ref.refs_7_, ...), custom_call_target="tpu_custom_call" | custom-call | tf_op jit(solution)/shard_map/pallas_call | solution.py:137
  111.0 1.3 broadcast_select_fusion.2
  112.3 0.9 broadcast_select_fusion.4
  113.2 1.3 broadcast_select_fusion
  114.5 111.6 %shard_map.215 = (f32[512,1024]{1,0:T(8,128)}, bf16[512,4096]{1,0:T(8,128)(2,1)}, bf16[512,512]{1,0:T(8,128)(2,1)}, bf16[512,2048]{1,0:T(8,128)(2,1)}, bf16[512,...) custom-call(bf16[512,2048]{1,0:T(8,128)(2,1)} %get-tuple-element.100, ...), custom_call_target="tpu_custom_call" | custom-call | tf_op jit(solution)/shard_map/pallas_call | solution.py:1379
  226.1 230.0 %shard_map.216 = (f32[128,4096]{1,0:T(8,128)}, f32[128,4096]{1,0:T(8,128)}, f32[128,1024]{1,0:T(8,128)}, f32[128,1024]{1,0:T(8,128)}, f32[128,1024]{1,0:T(8,128)...) custom-call(bf16[512,4096]{1,0:T(8,128)(2,1)} %get-tuple-element.132.refs_0_, ...), custom_call_target="tpu_custom_call" | custom-call | tf_op jit(solution)/shard_map/pallas_call | solution.py:1443
  456.2 2.6 shard_map.217
  460.0 2.0 copy.35
  464.5 1.3 copy.39
  465.8 1.0 copy-done.1
  466.8 1.3 copy.40
  468.1 1.0 copy-done
  469.1 1.3 copy.41
  (37 shorter events, 7.9 us)
Async XLA Ops:
  0.6 14.4 %copy-start.6 = (f32[512]{0:T(512)S(1)}, f32[512]{0:T(512)}, u32[]{:S(2)}) copy-start(f32[512]{0:T(512)} %param.21) | copy-start | bytes 6148
  0.7 14.3 %copy-start.7 = (f32[512]{0:T(512)S(1)}, f32[512]{0:T(512)}, u32[]{:S(2)}) copy-start(f32[512]{0:T(512)} %param.16) | copy-start | bytes 6148
  1.4 13.6 %collective-permute-start = (f32[2,512]{1,0:T(2,128)S(1)}, f32[2,512]{1,0:T(2,128)S(1)}, u32[]{:S(2)}, u32[]{:S(2)}) collective-permute-start(f32[2,512]{1,0:T(2,128)S(1)} %pad_maximum_fusion.10), channel_id=1, source_target_pairs={{0,1},{1,0},{2,3},{3,2},{4,5},{5,4},{6,7},{7,6},{8,9},{9,8},{10,11... | collective-permute-start | bytes 12296 | tf_op jit(solution)/shard_map/ppermute | solution.py:1532
  15.0 1.3 collective-permute-start.1
  456.1 5.9 %copy-start.5 = (f32[128,1024]{1,0:T(8,128)S(1)}, f32[128,1024]{1,0:T(8,128)}, u32[]{:S(2)}) copy-start(f32[128,1024]{1,0:T(8,128)} %get-tuple-element.216) | copy-start | bytes 1572868
  456.1 6.7 %copy-start.4 = (f32[128,1024]{1,0:T(8,128)S(1)}, f32[128,1024]{1,0:T(8,128)}, u32[]{:S(2)}) copy-start(f32[128,1024]{1,0:T(8,128)} %get-tuple-element.217) | copy-start | bytes 1572868
  456.2 7.5 %copy-start.3 = (f32[128,1024]{1,0:T(8,128)S(1)}, f32[128,1024]{1,0:T(8,128)}, u32[]{:S(2)}) copy-start(f32[128,1024]{1,0:T(8,128)} %get-tuple-element.218) | copy-start | bytes 1572868
  460.0 4.4 copy-start.2
  464.5 2.3 copy-start.1
  466.8 2.3 copy-start

commit v2 on v1

--- a/solution.py
+++ b/solution.py
@@ -115,38 +115,6 @@
         turn_back(dk * scale, cos, first, second).astype(BF16),
         dv.astype(BF16),
     )
-
-
-def feed_kernel(x_ref, gate_ref, up_ref, da_ref, hidden_ref, dg_ref, du_ref):
-    x = x_ref[...]
-    gate = mm(x, gate_ref[...])
-    up = mm(x, up_ref[...])
-    da = da_ref[...]
-    sigmoid = 1.0 / (1.0 + jnp.exp(-gate))
-    swish = gate * sigmoid
-    hidden_ref[...] = (swish * up).astype(BF16)
-    dg_ref[...] = (da * up * sigmoid * (1.0 + gate * (1.0 - sigmoid))).astype(BF16)
-    du_ref[...] = (da * swish).astype(BF16)
-
-
-def feed_forward(x, pair_w, hidden_grad, tile=256):
-    height, depth = x.shape
-    width = hidden_grad.shape[1]
-    steps = width // tile
-    tall = pl.BlockSpec((height, tile), lambda j: (0, j))
-    return pl.pallas_call(
-        feed_kernel,
-        out_shape=(jax.ShapeDtypeStruct((height, width), BF16),) * 3,
-        grid=(steps,),
-        in_specs=[
-            whole(x.shape),
-            pl.BlockSpec((depth, tile), lambda j: (0, j)),
-            pl.BlockSpec((depth, tile), lambda j: (0, j + steps)),
-            tall,
-        ],
-        out_specs=(tall,) * 3,
-        cost_estimate=FREE,
-    )(x, pair_w, pair_w, hidden_grad)
 
 
 MESH = pl.DeviceIdType.MESH
@@ -540,8 +508,9 @@
     lax.fori_loop(0, ROWS // size, one, 0)
 
 
-def deal_kernel(order_ref, tokens_ref, dealt_ref):
+def prepare_kernel(order_ref, len_ref, tokens_ref, top_ref, dealt_ref, block_ref, live_ref):
     groups = tokens_ref.shape[1]
+    dp = lax.axis_index("dp")
 
     def one(at, _):
         micro, slot = at // groups, lax.rem(at, groups)
@@ -549,17 +518,30 @@
         return 0
 
     lax.fori_loop(0, MICRO * groups, one, 0)
-
-
-def deal(order, tokens):
+    for micro in range(MICRO):
+        length = len_ref[micro, order_ref[micro, dp]]
+        rows = lax.broadcasted_iota(jnp.int32, top_ref.shape[2:], 0)
+        top = top_ref[micro, 0]
+        top = jnp.where(rows < length, top.astype(F32), 0.0).astype(BF16)
+        block_ref[micro * SL : micro * SL + SL, :] = top
+        keys = lax.broadcasted_iota(jnp.int32, (1, SL), 1)
+        live_ref[micro : micro + 1, :] = jnp.where(keys < length, 1.0, 0.0)
+
+
+def prepare(order, lengths, tokens, cotangent):
     vmem = pl.BlockSpec(memory_space=pltpu.VMEM)
+    smem = pl.BlockSpec(memory_space=pltpu.SMEM)
     return pl.pallas_call(
-        deal_kernel,
-        out_shape=jax.ShapeDtypeStruct(tokens.shape, BF16),
-        in_specs=[pl.BlockSpec(memory_space=pltpu.SMEM), vmem],
-        out_specs=vmem,
+        prepare_kernel,
+        out_shape=(
+            jax.ShapeDtypeStruct(tokens.shape, BF16),
+            jax.ShapeDtypeStruct((ROWS, cotangent.shape[3]), BF16),
+            jax.ShapeDtypeStruct((MICRO, SL), F32),
+        ),
+        in_specs=[smem, smem, vmem, vmem],
+        out_specs=(vmem,) * 3,
         cost_estimate=FREE,
-    )(order, tokens)
+    )(order, lengths, tokens, cotangent)
 
 
 def front_kernel(
@@ -593,8 +575,12 @@
     inverse_second,
     normed_second,
     hidden_grad,
+    gains,
     qkv_w,
     out_w,
+    gains_own,
+    gains_col,
+    gains_row,
     pair_held,
     down_held,
     tiles,
@@ -689,6 +675,9 @@
             return 0
 
         lax.fori_loop(1, groups, send_rows, 0)
+    gains_own[0:1, :] = gain_first[...]
+    gains_own[1:2, :] = gain_second[...]
+    gain_c = swap(gains_own, gains_col, 13, beside)
     top_c = swap(top_block, top_col, 0, beside)
     weights_now = []
     for kind, w in enumerate((query_weight, key_weight, value_weight)):
@@ -738,6 +727,9 @@
 
         lax.fori_loop(1, groups, take_rows, 0)
         x_c.append(swap(x_in.at[micro], x_came.at[micro], 1 + micro, beside))
+    gain_c.wait_recv()
+    gains[...] = half_of(gains_own[...], gains_col[...])
+    gain_r = swap(gains, gains_row, 14, across)
     top_c.wait_recv()
 
     def top_rows(rows):
@@ -774,7 +766,9 @@
         jnp.int32, (SL, SL), 0
     )
 
-    def norm_rows(own_ref, other_ref, gain, inverse_ref, out_ref, micro):
+    gain_r.wait_recv()
+
+    def norm_rows(own_ref, other_ref, at, inverse_ref, out_ref, micro):
         def body(j, _):
             rows = pl.ds(pl.multiple_of(micro * SL + j * 64, 64), 64)
             own = own_ref[rows, :].astype(F32)
@@ -783,8 +777,8 @@
             total = total + jnp.sum(other * other, axis=1, keepdims=True)
             inverse = lax.rsqrt(total / D + EPSILON)
             inverse_ref[rows, :] = inverse
-            out_ref[rows, :half] = (own * inverse * gain[:, :half]).astype(BF16)
-            out_ref[rows, half:] = (other * inverse * gain[:, half:]).astype(BF16)
+            out_ref[rows, :half] = (own * inverse * gains[at : at + 1, :]).astype(BF16)
+            out_ref[rows, half:] = (other * inverse * gains_row[at : at + 1, :]).astype(BF16)
             return 0
 
         lax.fori_loop(0, SL // 64, body, 0)
@@ -793,7 +787,7 @@
     for micro in range(MICRO):
         rows = micro_rows(micro)
         x_r[micro].wait_recv()
-        norm_rows(x_half, x_other, gain_first, inverse_first, normed_first, micro)
+        norm_rows(x_half, x_other, 0, inverse_first, normed_first, micro)
         allowed = lower & (key_live[micro : micro + 1, :] > 0.5)
 
         def attend(at, _):
@@ -851,7 +845,7 @@
         lax.fori_loop(0, SL // 64, middle_rows, 0)
         low_r.append(swap(low.at[rows, :], low_came.at[rows, :], 11 + micro, across))
         low_r[micro].wait_recv()
-        norm_rows(low, low_came, gain_second, inverse_second, normed_second, micro)
+        norm_rows(low, low_came, 1, inverse_second, normed_second, micro)
 
     top_x.wait_recv()
     for copy in weights_late:
@@ -904,12 +898,16 @@
             array(ROWS, 1, dtype=F32),
             array(ROWS, D),
             array(ROWS, quarter, dtype=F32),
+            array(2, half, dtype=F32),
         ],
         in_specs=[vmem] * 8 + [anywhere] * 7,
-        out_specs=[anywhere] * 4 + [vmem] * 11,
+        out_specs=[anywhere] * 4 + [vmem] * 12,
         scratch_shapes=[
             buffer(D, 3 * heads),
             buffer(heads, D),
+            buffer(2, block, dtype=F32),
+            buffer(2, block, dtype=F32),
+            buffer(2, half, dtype=F32),
             buffer(2, half, quarter),
             buffer(quarter, half),
             buffer(2, 256, D),
@@ -928,7 +926,7 @@
             sem((2, MICRO, groups)),
             sem((2, now + 3)),
             sem((now + 9,)),
-            sem((2, 13)),
+            sem((2, 15)),
             sem((2, 2)),
         ],
         compiler_params=pltpu.CompilerParams(
@@ -940,9 +938,8 @@
 
 def chain_kernel(
     line,
-    hidden,
-    gate_grad,
-    up_grad,
+    normed,
+    hidden_grad,
     second_mine,
     second_theirs,
     top_half,
@@ -965,6 +962,7 @@
     down_out,
     gate_grads,
     second_came,
+    up_grad,
     up_row,
     dqkv,
     dqkv_row,
@@ -974,9 +972,11 @@
     gate_row,
     gate_came,
     gate_came_row,
+    hidden,
+    gate_grad,
     tiles,
     tall_tiles,
-    pair_tiles,
+    da_tiles,
     kept,
     sent,
     row_came,
@@ -1012,7 +1012,7 @@
     down_line = ZLine(line, down_grads, down_out, None, down_z, down_sems, 4, True)
     half = D // 2
     block = D // 4
-    quarter = hidden.shape[1]
+    quarter = normed.shape[1]
     pending = []
 
     def swap(source, target, at, device, sems=swap_sems):
@@ -1040,16 +1040,63 @@
 
     per = line // 2
     width = quarter // line
+    tile = min(width, 256)
+    each = width // tile
 
     def hidden_part(index, at):
         return hidden.at[:, pl.ds(pl.multiple_of((2 * at + index) * width, width), width)]
 
-    to_x, to_row, on_row = [], [], []
-    for at in range(per):
-        there = pl.ds(at * width, width)
-        to_x.append(
-            begin(swap(hidden_part(1 - x, at), hidden_came.at[:, there], at, partner, piece_sems))
-        )
+    def feed_columns(j, shift=0):
+        piece = j // each
+        index = jnp.where(piece < per, 1 - x, x)
+        begin = (2 * lax.rem(piece, per) + index) * width + lax.rem(j, each) * tile
+        return pl.ds(pl.multiple_of(shift + begin, tile), tile)
+
+    to_x = [
+        swap(
+            hidden_part(1 - x, at),
+            hidden_came.at[:, pl.ds(at * width, width)],
+            at,
+            partner,
+            piece_sems,
+        )
+        for at in range(per)
+    ]
+    pending.extend(to_x)
+
+    def feed_body(j, slot):
+        gate = mm(normed[...], tall_tiles[slot, 0, :, :tile])
+        up = mm(normed[...], tall_tiles[slot, 1, :, :tile])
+        da = da_tiles[slot, :, :tile]
+        sigmoid = 1.0 / (1.0 + jnp.exp(-gate))
+        swish = gate * sigmoid
+        there = feed_columns(j)
+        hidden[:, there] = (swish * up).astype(BF16)
+        gate_grad[:, there] = (da * up * sigmoid * (1.0 + gate * (1.0 - sigmoid))).astype(BF16)
+        up_grad[:, there] = (da * swish).astype(BF16)
+        for at in range(per):
+
+            @pl.when(j == (at + 1) * each - 1)
+            def _():
+                to_x[at].start()
+
+    narrow_tile = pl.ds(0, tile)
+    stream(
+        lambda j: [
+            pair_w.at[:, feed_columns(j)],
+            pair_w.at[:, feed_columns(j, quarter)],
+            hidden_grad.at[:, feed_columns(j)],
+        ],
+        lambda slot: [
+            tall_tiles.at[slot, 0, :, narrow_tile],
+            tall_tiles.at[slot, 1, :, narrow_tile],
+            da_tiles.at[slot, :, narrow_tile],
+        ],
+        tile_sems,
+        quarter // tile,
+        feed_body,
+    )
+    to_row, on_row = [], []
     for at in range(per):
         there = pl.ds(at * width, width)
         to_row.append(
@@ -1093,11 +1140,11 @@
 
     def down_product(start, target, dtype):
         def body(j, slot):
-            target[:, columns_at(j)] = mm(hidden[...], tall_tiles[slot]).astype(dtype)
+            target[:, columns_at(j)] = mm(hidden[...], tall_tiles[slot, 0]).astype(dtype)
 
         stream(
             lambda j: [down_w.at[:, pl.ds(pl.multiple_of(start + j * 256, 256), 256)]],
-            lambda slot: [tall_tiles.at[slot]],
+            lambda slot: [tall_tiles.at[slot, 0]],
             tile_sems,
             half // 256,
             body,
@@ -1164,7 +1211,7 @@
 
     def second_grads(rows):
         grad = summed[rows, :].astype(F32) + col_came[rows, :].astype(F32)
-        return grad, grad * gain_second[...]
+        return grad, grad * gain_second[1:2, :]
 
     def norm_first_pass(rows):
         grad, scaled = second_grads(rows)
@@ -1271,28 +1318,28 @@
         def body(j, slot):
             mine, came = values(j, slot)
             total = mm(turned_left[:, :depth], mine) + mm(turned_left[:, depth:], came)
-            there = pl.ds(pl.multiple_of(shift + j * 512, 512), 512)
+            there = pl.ds(pl.multiple_of(shift + j * 256, 256), 256)
             gate_grads[:, there] = total.astype(BF16)
 
         stream(
-            lambda j: [source.at[:, columns_at(j, 512)] for source in sources],
-            lambda slot: [pair_tiles.at[slot, k] for k in range(len(sources))],
+            lambda j: [source.at[:, columns_at(j)] for source in sources],
+            lambda slot: [tall_tiles.at[slot, k, pl.ds(0, ROWS)] for k in range(len(sources))],
             tile_sems,
-            quarter // 512,
+            quarter // 256,
             body,
         )
 
     gate_part(
         0,
         [gate_came],
-        lambda j, slot: (gate_grad[:, columns_at(j, 512)], pair_tiles[slot, 0]),
+        lambda j, slot: (gate_grad[:, columns_at(j)], tall_tiles[slot, 0, :ROWS]),
     )
     gate_r.wait_recv()
     gate_on.wait_recv()
     gate_part(
         quarter,
         [gate_row, gate_came_row],
-        lambda j, slot: (pair_tiles[slot, 0], pair_tiles[slot, 1]),
+        lambda j, slot: (tall_tiles[slot, 0, :ROWS], tall_tiles[slot, 1, :ROWS]),
     )
 
     layer_c.wait_recv()
@@ -1345,15 +1392,14 @@
 
 
 def chain(line, identity, *values):
-    hidden, gate_grad = values[:2]
-    quarter = hidden.shape[1]
-    narrow = values[3].shape[1]
-    qkv_width = values[11].shape[1]
+    quarter = values[1].shape[1]
+    narrow = values[2].shape[1]
+    qkv_width = values[10].shape[1]
     half, block = D // 2, D // 4
     rows = quarter // 2
     vmem = pl.BlockSpec(memory_space=pltpu.VMEM)
     anywhere = pl.BlockSpec(memory_space=pl.ANY)
-    outside = {7, 8, 9, 10, 12}
+    outside = {1, 3, 6, 7, 8, 9, 11}
 
     def array(*shape, dtype=BF16):
         return jax.ShapeDtypeStruct(shape, dtype)
@@ -1365,6 +1411,7 @@
         (array(2 * rows // line, half, dtype=F32), anywhere),
         (array(narrow, 2 * quarter), vmem),
         (array(ROWS, narrow), vmem),
+        (array(ROWS, quarter), vmem),
         (array(ROWS, quarter), anywhere),
         (array(ROWS, qkv_width), vmem),
         (array(ROWS, qkv_width), anywhere),
@@ -1382,9 +1429,11 @@
         in_specs=[anywhere if k in outside else vmem for k in range(len(values))],
         out_specs=[place for _, place in outs],
         scratch_shapes=[
+            buffer(ROWS, quarter),
+            buffer(ROWS, quarter),
             buffer(2, 256, 2 * quarter),
-            buffer(2, quarter, 256),
-            buffer(2, 2, ROWS, 512),
+            buffer(2, 2, quarter, 256),
+            buffer(2, ROWS, 256, dtype=F32),
             buffer(ROWS, half, dtype=F32),
             buffer(ROWS, half),
             buffer(3, ROWS, half),
@@ -1408,7 +1457,7 @@
             buffer(1, block, dtype=F32),
             sem((2, 17)),
             sem((2, 3 * (line // 2))),
-            sem((2, 2)),
+            sem((2, 3)),
             sem((2, 2, line - 1, 4)),
             sem((2,)),
         ],
@@ -1476,8 +1525,15 @@
     )(*values)
 
 
-def put_back_kernel(order_ref, back_ref, layer_ref, grad_ref):
+def finish_kernel(count, order_ref, back_ref, *refs):
+    sums, rest = refs[:count], refs[count:]
+    layer_ref, grad_ref = rest[:2]
+    outs, held, sems = rest[2 : 2 + count], rest[2 + count : 2 + 2 * count], rest[2 + 2 * count]
     groups = back_ref.shape[1]
+    loads = [pltpu.make_async_copy(sums[k], held[k], sems.at[0, k]) for k in range(count)]
+    stores = [pltpu.make_async_copy(held[k], outs[k], sems.at[1, k]) for k in range(count)]
+    for copy in loads:
+        copy.start()
 
     def one(at, _):
         micro, slot = at // groups, lax.rem(at, groups)
@@ -1487,18 +1543,27 @@
         return 0
 
     lax.fori_loop(0, MICRO * groups, one, 0)
-
-
-def put_back(order, back):
+    for load, store in zip(loads, stores):
+        load.wait()
+        store.start()
+    for store in stores:
+        store.wait()
+
+
+def finish(order, back, *sums):
     vmem = pl.BlockSpec(memory_space=pltpu.VMEM)
-    shape = jax.ShapeDtypeStruct((MICRO,) + back.shape[1:], BF16)
+    anywhere = pl.BlockSpec(memory_space=pl.ANY)
+    rows = jax.ShapeDtypeStruct((MICRO,) + back.shape[1:], BF16)
+    count = len(sums)
     return pl.pallas_call(
-        put_back_kernel,
-        out_shape=(shape, shape),
-        in_specs=[pl.BlockSpec(memory_space=pltpu.SMEM), vmem],
-        out_specs=(vmem, vmem),
+        lambda *refs: finish_kernel(count, *refs),
+        out_shape=[rows, rows] + [jax.ShapeDtypeStruct(v.shape, F32) for v in sums],
+        in_specs=[pl.BlockSpec(memory_space=pltpu.SMEM), vmem] + [anywhere] * count,
+        out_specs=[vmem, vmem] + [anywhere] * count,
+        scratch_shapes=[pltpu.VMEM(v.shape, F32) for v in sums]
+        + [pltpu.SemaphoreType.DMA((2, count))],
         cost_estimate=FREE,
-    )(order, back)
+    )(order, back, *sums)
 
 
 def per_device(
@@ -1547,25 +1612,11 @@
         )
         return jnp.where(x == 0, even, odd), jnp.where(x == 0, odd, even)
 
-    token = []
-
-    def ordered_after(*values):
-        out = lax.optimization_barrier(tuple(values) + tuple(token))
-        return out[: len(values)] if len(values) > 1 else out[0]
-
-    def mark(value):
-        token[:] = [value]
-        return value
-
-    own_order = lax.dynamic_slice_in_dim(deal_order, dp, 1, 1)
-    own_lengths = jnp.take_along_axis(lengths, own_order, axis=1)[:, 0]
+    def plain(*values):
+        return values
+
+    dealt, top_block, key_live = prepare(deal_order, lengths, tokens, cotangent)
     tables = rope_tables()
-    live = (jnp.arange(SL, dtype=jnp.int32)[None, :] < own_lengths[:, None]).reshape(ROWS, 1)
-    key_live = live.reshape(MICRO, SL).astype(F32)
-    top_block = jnp.where(live, cotangent.reshape(ROWS, block), 0.0).astype(BF16)
-    gains = jnp.stack([attention_gain, feed_gain])
-    gains_half = ordered(gains, over_col(gains), col)
-    gains_full = jnp.concatenate([gains_half, over_row(gains_half)], axis=1)
     (
         pair_w,
         down_w,
@@ -1582,13 +1633,14 @@
         inverse_second,
         normed_second,
         hidden_grad,
+        gains_half,
     ) = front(
         line,
         0,
-        deal(deal_order, tokens),
+        dealt,
         top_block,
-        gains_full[:1],
-        gains_full[1:],
+        attention_gain.reshape(1, block),
+        feed_gain.reshape(1, block),
         key_live,
         *tables,
         query_weight,
@@ -1601,12 +1653,6 @@
     )
     x_block = x_block.reshape(ROWS, block)
     narrow = half // groups
-    hidden, gate_grad, up_grad = feed_forward(normed_second, pair_w, hidden_grad)
-    mark(hidden)
-
-    def own_block(v):
-        return lax.dynamic_slice_in_dim(v, col * block, block, 1)
-
     first_mine, first_theirs = x_parts(normed_first[:, :half], narrow)
     mixed_mine, mixed_theirs = x_parts(mixed, 2 * mixed.shape[1] // groups)
     second_mine, second_theirs = x_parts(normed_second[:, :half], narrow)
@@ -1614,6 +1660,7 @@
         down_sum,
         gate_grads,
         second_came,
+        up_grad,
         up_row,
         dqkv,
         dqkv_row,
@@ -1626,10 +1673,9 @@
     ) = chain(
         line,
         4,
-        *ordered_after(
-            hidden,
-            gate_grad,
-            up_grad,
+        *plain(
+            normed_second,
+            hidden_grad,
             second_mine,
             second_theirs,
             top_half,
@@ -1642,19 +1688,18 @@
             middle,
             inverse_first,
             inverse_second,
-            gains_half[1:],
-            own_block(gains_half)[:1],
+            gains_half,
+            attention_gain.reshape(1, block),
             x_block,
             key_live,
             *tables,
         ),
     )
-    mark(both)
 
     gate_sum, up_sum, query_sum, key_sum, value_sum, output_sum, back, gain_sums = tail_sums(
         line,
         3,
-        *ordered_after(
+        *plain(
             gate_grads,
             up_grad,
             up_row,
@@ -1671,7 +1716,27 @@
             pieces,
         ),
     )
-    layer_output, tokens_grad = put_back(deal_order, back)
+    (
+        layer_output,
+        tokens_grad,
+        down_sum,
+        gate_sum,
+        up_sum,
+        query_sum,
+        key_sum,
+        value_sum,
+        output_sum,
+    ) = finish(
+        deal_order,
+        back,
+        down_sum,
+        gate_sum,
+        up_sum,
+        query_sum,
+        key_sum,
+        value_sum,
+        output_sum,
+    )
     gain_size = block // groups
     gain_sums = lax.dynamic_slice_in_dim(gain_sums, dp * gain_size, gain_size, 1)
 

time: 472 us -> 451 us (0.956)
  local copies, waits for them, and re-layouts: 17.4 us -> 3.18 us
  other arithmetic: 11.8 us -> 5.14 us
    pallas_call x3 -> x2, Pallas kernels: 21.8 us -> 11 us  [the longest x1 8.57 us: finish(): pl.pallas_call(lambda *refs: finish_kernel(count, *refs), out_shape=[rows...]
    pallas_call x1, Pallas kernels: 112 us -> 122 us  [chain(): pl.pallas_call(lambda *refs: chain_kernel(line, *refs), out_shape=[shape...]
    unnamed x24 -> x4, local copies, waits for them, and re-layouts: 10.5 us -> 0.25 us
  transfers between devices with their start and end apart: 2 -> 0, of which waited for: 0 -> 0; matrix products, arithmetic and copies ran while one was open for 2% -> 0% of each run, Pallas kernels for 0% -> 0%
where the time goes in v2:
time: 451 us; the launch traced here: 450 us
  Pallas kernels  441 us (98%)
  other arithmetic  5.14 us (1%)
    pallas_call x1, Pallas kernels, tail_sums(): pl.pallas_call(lambda *refs: tail_kernel(line, *refs), out_shape=[array(*...  234 us
    pallas_call x1, Pallas kernels, chain(): pl.pallas_call(lambda *refs: chain_kernel(line, *refs), out_shape=[shape...  122 us
    pallas_call x1, Pallas kernels, front(): pl.pallas_call(front_kernel, out_shape=[array(D, 2 * quarter), array(quar...  73.9 us

profile of v2, /device:TPU:0, one launch (start us, length us, event | category | flops | bytes accessed | tf_op | source)
XLA Modules:
  0.0 449.7 jit_solution(925901213714278446)
XLA Ops:
  0.7 0.5 fusion
  1.2 1.1 pad_maximum_fusion.8
  2.3 2.4 shard_map.212
  4.8 73.9 %shard_map.213 = (bf16[2048,4096]{1,0:T(8,128)(2,1)}, bf16[2048,2048]{1,0:T(8,128)(2,1)}, bf16[2048,1536]{1,0:T(8,128)(2,1)}, bf16[512,2048]{1,0:T(8,128)(2,1)},...) custom-call(bf16[2,8,32,512]{3,2,1,0:T(8,128)(2,1)} %get-tuple-eleme, ...), custom_call_target="tpu_custom_call" | custom-call | tf_op jit(solution)/shard_map/pallas_call | solution.py:883
  78.7 0.0 copy-start.1
  78.7 1.3 fusion.4
  80.0 0.9 broadcast_select_fusion.4
  80.9 0.0 copy-done.1
  80.9 0.0 copy-start
  80.9 0.2 fusion.2
  81.1 1.3 broadcast_select_fusion
  82.4 0.2 copy-done
  82.7 0.2 fusion.3
  82.9 1.3 broadcast_select_fusion.2
  84.2 122.1 %shard_map.214 = (f32[512,1024]{1,0:T(8,128)}, bf16[512,4096]{1,0:T(8,128)(2,1)}, bf16[512,512]{1,0:T(8,128)(2,1)}, bf16[512,2048]{1,0:T(8,128)(2,1)}, bf16[512,...) custom-call(bf16[512,2048]{1,0:T(8,128)(2,1)} %get-tuple-element.60., ...), custom_call_target="tpu_custom_call" | custom-call | tf_op jit(solution)/shard_map/pallas_call | solution.py:1426
  206.3 233.5 %shard_map.215 = (f32[128,4096]{1,0:T(8,128)}, f32[128,4096]{1,0:T(8,128)}, f32[128,1024]{1,0:T(8,128)}, f32[128,1024]{1,0:T(8,128)}, f32[128,1024]{1,0:T(8,128)...) custom-call(bf16[512,4096]{1,0:T(8,128)(2,1)} %get-tuple-element.74.refs_0_, ...), custom_call_target="tpu_custom_call" | custom-call | tf_op jit(solution)/shard_map/pallas_call | solution.py:1492
  439.9 8.6 %shard_map.216 = (bf16[2,8,32,512]{3,2,1,0:T(8,128)(2,1)}, bf16[2,8,32,512]{3,2,1,0:T(8,128)(2,1)}, f32[512,1024]{1,0:T(8,128)}, f32[128,4096]{1,0:T(8,128)}, f3...) custom-call(s32[2,8]{1,0:T(2,128)} %refs_0_.1, ...), custom_call_target="tpu_custom_call" | custom-call | tf_op jit(solution)/shard_map/pallas_call | solution.py:1558
  448.4 0.7 constant_dynamic-slice_fusion
  449.2 0.5 slice_bitcast_fusion
  (2 shorter events, 0.0 us)
Async XLA Ops:
  78.7 2.2 copy-start.1
  80.9 1.8 copy-start

commit v3 on v2

--- a/solution.py
+++ b/solution.py
@@ -235,16 +235,16 @@
 def tail_kernel(
     line,
     gate_grads,
-    up,
-    up_row,
-    second_mine,
-    second_came,
-    dqkv,
-    dqkv_row,
-    first_mine,
+    up_in,
+    up_row_in,
+    second_mine_in,
+    second_came_in,
+    dqkv_in,
+    dqkv_row_in,
+    first_mine_in,
     first_theirs,
-    branch,
-    mixed_mine,
+    branch_in,
+    mixed_mine_in,
     mixed_theirs,
     both,
     pieces,
@@ -256,6 +256,15 @@
     output_out,
     back,
     gains_out,
+    up,
+    up_row,
+    second_mine,
+    second_came,
+    dqkv,
+    dqkv_row,
+    first_mine,
+    branch,
+    mixed_mine,
     gate_z,
     up_z,
     qkv_z,
@@ -286,6 +295,7 @@
     gains,
     back_sems,
     gain_sems,
+    fetch_sems,
 ):
     groups = 2 * line
     dp, row = lax.axis_index("dp"), lax.axis_index("row")
@@ -305,14 +315,29 @@
             device_id_type=MESH,
         )
 
-    up_x = swap(up, up_came, 0, {"dp": partner})
-    branch_x = swap(branch, branch_came, 1, {"dp": partner})
-    dqkv_x = swap(dqkv, dqkv_came, 2, {"dp": partner})
+    fetches = {}
+    order = (
+        (second_mine_in, second_mine),
+        (second_came_in, second_came),
+        (up_in, up),
+        (up_row_in, up_row),
+        (mixed_mine_in, mixed_mine),
+        (branch_in, branch),
+        (first_mine_in, first_mine),
+        (dqkv_in, dqkv),
+        (dqkv_row_in, dqkv_row),
+    )
+    for at, (source, target) in enumerate(order):
+        fetches[at] = pltpu.make_async_copy(source, target, fetch_sems.at[at])
+        fetches[at].start()
+    up_x = swap(up_in, up_came, 0, {"dp": partner})
+    branch_x = swap(branch_in, branch_came, 1, {"dp": partner})
+    dqkv_x = swap(dqkv_in, dqkv_came, 2, {"dp": partner})
     up_across = swap(up_came, up_came_row, 3, {"row": 1 - row})
     dqkv_across = swap(dqkv_came, dqkv_came_row, 4, {"row": 1 - row})
     first_x = swap(first_theirs, first_came, 5, {"dp": partner})
     mixed_x = swap(mixed_theirs, mixed_came, 6, {"dp": partner})
-    mixed_r = swap(mixed_mine, mixed_row, 7, {"row": 1 - row})
+    mixed_r = swap(mixed_mine_in, mixed_row, 7, {"row": 1 - row})
     mixed_across = swap(mixed_came, mixed_came_row, 8, {"row": 1 - row})
 
     stores = []
@@ -394,6 +419,8 @@
     lax.fori_loop(1, groups, send_back, 0)
     store(both.at[:, dp], back.at[:, dp])
 
+    fetches[0].wait()
+    fetches[1].wait()
     depth = second_mine.shape[0]
     turned_left[:, :depth] = second_mine[...].T
     turned_left[:, depth:] = second_came[...].T
@@ -412,6 +439,8 @@
     up_across.start()
     gain_step(0)
     gate_line.run(2, line - 1)
+    fetches[2].wait()
+    fetches[3].wait()
     wide(up_grads, 0, up, up_came)
     up_across.wait_recv()
     wide(up_grads, up.shape[1], up_row, up_came_row)
@@ -430,6 +459,8 @@
 
         tiles_loop(branch.shape[1], 512, body)
 
+    fetches[4].wait()
+    fetches[5].wait()
     side(0, mixed_mine, mixed_came)
     mixed_r.wait_recv()
     mixed_across.wait_recv()
@@ -437,6 +468,8 @@
     output_line.run(0, 1)
     up_line.run(1, 2)
     gain_step(1)
+    for at in (6, 7, 8):
+        fetches[at].wait()
     first_x.wait_recv()
     turned_left[:, :depth] = first_mine[...].T
     turned_left[:, depth:] = first_came[...].T
@@ -564,18 +597,37 @@
     down_out,
     qkv_out,
     out_out,
+    x_out,
+    top_half_out,
+    top_came_out,
+    first_mine_out,
+    first_theirs_out,
+    turned_out,
+    mixed_mine_out,
+    mixed_theirs_out,
+    middle_out,
+    second_mine_out,
+    second_theirs_out,
+    normed_second_out,
+    hidden_grad_out,
+    inverse_first,
+    inverse_second,
+    gains,
     x_in,
     top_half,
     top_came,
     normed_first,
+    first_mine,
+    first_theirs,
     turned,
     mixed,
+    mixed_mine,
+    mixed_theirs,
     middle,
-    inverse_first,
-    inverse_second,
+    second_mine,
+    second_theirs,
     normed_second,
     hidden_grad,
-    gains,
     qkv_w,
     out_w,
     gains_own,
@@ -604,7 +656,8 @@
 ):
     groups = dealt.shape[1]
     dp, row, col = lax.axis_index("dp"), lax.axis_index("row"), lax.axis_index("col")
-    partner = {"dp": dp + 1 - 2 * lax.rem(dp, 2)}
+    x = lax.rem(dp, 2)
+    partner = {"dp": dp + 1 - 2 * x}
     across = {"row": 1 - row}
     beside = {"col": 1 - col}
     half, block = D // 2, D // 4
@@ -736,6 +789,7 @@
         top_half[rows, :] = half_of(top_block[rows, :], top_col[rows, :])
 
     rows_loop(top_rows)
+    results = [local(x_in, x_out), local(top_half, top_half_out)]
     top_x = swap(top_half, top_came, 3, partner)
 
     def micro_rows(micro):
@@ -811,6 +865,16 @@
         summed[rows, :] = (kept[...] + row_came[rows, :].astype(F32)).astype(BF16)
         sum_c.append(swap(summed.at[rows, :], col_came.at[rows, :], 9 + micro, beside))
 
+    results.append(local(turned, turned_out))
+
+    def by_x(source, mine, theirs, rows, width):
+        value = source[rows, : 2 * mine.shape[1]]
+        even = [value[:, at : at + width] for at in range(0, value.shape[1], 2 * width)]
+        odd = [value[:, at : at + width] for at in range(width, value.shape[1], 2 * width)]
+        even, odd = jnp.concatenate(even, axis=1), jnp.concatenate(odd, axis=1)
+        mine[rows, :] = jnp.where(x == 0, even, odd)
+        theirs[rows, :] = jnp.where(x == 0, odd, even)
+
     top_r.wait_recv()
     store_down.wait()
     down_r.wait_recv()
@@ -827,6 +891,18 @@
         quarter // 256,
         da_body,
     )
+
+    results.append(local(hidden_grad, hidden_grad_out))
+
+    def select_rows(rows):
+        by_x(normed_first, first_mine, first_theirs, rows, half // groups)
+        by_x(mixed, mixed_mine, mixed_theirs, rows, 2 * heads // groups)
+
+    rows_loop(select_rows)
+    results.append(local(first_mine, first_mine_out))
+    results.append(local(first_theirs, first_theirs_out))
+    results.append(local(mixed_mine, mixed_mine_out))
+    results.append(local(mixed_theirs, mixed_theirs_out))
 
     low_r = []
     for micro in range(MICRO):
@@ -843,11 +919,23 @@
             return 0
 
         lax.fori_loop(0, SL // 64, middle_rows, 0)
+        results.append(local(middle.at[rows, :], middle_out.at[rows, :]))
         low_r.append(swap(low.at[rows, :], low_came.at[rows, :], 11 + micro, across))
         low_r[micro].wait_recv()
         norm_rows(low, low_came, 1, inverse_second, normed_second, micro)
+        results.append(local(normed_second.at[rows, :], normed_second_out.at[rows, :]))
+
+        def second_rows(j, _):
+            here = pl.ds(pl.multiple_of(micro * SL + j * 64, 64), 64)
+            by_x(normed_second, second_mine, second_theirs, here, half // groups)
+            return 0
+
+        lax.fori_loop(0, SL // 64, second_rows, 0)
+        results.append(local(second_mine.at[rows, :], second_mine_out.at[rows, :]))
+        results.append(local(second_theirs.at[rows, :], second_theirs_out.at[rows, :]))
 
     top_x.wait_recv()
+    results.append(local(top_came, top_came_out))
     for copy in weights_late:
         copy.wait_recv()
     for copy in pending:
@@ -859,7 +947,7 @@
         return 0
 
     lax.fori_loop(1, groups, close, 0)
-    for copy in (store_gate, store_up, store_qkv, store_out):
+    for copy in [store_gate, store_up, store_qkv, store_out] + results:
         copy.wait()
 
 
@@ -880,6 +968,23 @@
 
     sem = pltpu.SemaphoreType.DMA
     now = 3 * (heads // 128) + 1
+    held = [
+        (dealt.shape, BF16),
+        ((ROWS, half), BF16),
+        ((ROWS, half), BF16),
+        ((ROWS, block), BF16),
+        ((ROWS, block), BF16),
+        ((ROWS, 3 * heads), BF16),
+        ((ROWS, heads // 2), BF16),
+        ((ROWS, heads // 2), BF16),
+        ((ROWS, half), F32),
+        ((ROWS, block), BF16),
+        ((ROWS, block), BF16),
+        ((ROWS, D), BF16),
+        ((ROWS, quarter), F32),
+    ]
+    normed_first, mixed = ((ROWS, D), BF16), ((ROWS, heads), BF16)
+    inside = held[:3] + [normed_first] + held[3:6] + [mixed] + held[6:]
     return pl.pallas_call(
         front_kernel,
         out_shape=[
@@ -887,22 +992,15 @@
             array(quarter, D),
             array(D, 3 * heads),
             array(heads, D),
-            array(*dealt.shape),
-            array(ROWS, half),
-            array(ROWS, half),
-            array(ROWS, D),
-            array(ROWS, 3 * heads),
-            array(ROWS, heads),
-            array(ROWS, half, dtype=F32),
+            *[array(*shape, dtype=kind) for shape, kind in held],
             array(ROWS, 1, dtype=F32),
             array(ROWS, 1, dtype=F32),
-            array(ROWS, D),
-            array(ROWS, quarter, dtype=F32),
             array(2, half, dtype=F32),
         ],
         in_specs=[vmem] * 8 + [anywhere] * 7,
-        out_specs=[anywhere] * 4 + [vmem] * 12,
+        out_specs=[anywhere] * (4 + len(held)) + [vmem] * 3,
         scratch_shapes=[
+            *[buffer(*shape, dtype=kind) for shape, kind in inside],
             buffer(D, 3 * heads),
             buffer(heads, D),
             buffer(2, block, dtype=F32),
@@ -925,7 +1023,7 @@
             buffer(ROWS, half),
             sem((2, MICRO, groups)),
             sem((2, now + 3)),
-            sem((now + 9,)),
+            sem((now + 28,)),
             sem((2, 15)),
             sem((2, 2)),
         ],
@@ -960,18 +1058,23 @@
     first,
     second,
     down_out,
-    gate_grads,
-    second_came,
-    up_grad,
+    gate_grads_out,
+    second_came_out,
+    up_grad_out,
     up_row,
-    dqkv,
+    dqkv_out,
     dqkv_row,
-    branch,
+    branch_out,
     both_out,
     pieces_out,
     gate_row,
     gate_came,
     gate_came_row,
+    gate_grads,
+    second_came,
+    up_grad,
+    dqkv,
+    branch,
     hidden,
     gate_grad,
     tiles,
@@ -1013,7 +1116,12 @@
     half = D // 2
     block = D // 4
     quarter = normed.shape[1]
-    pending = []
+    pending, results = [], []
+
+    def result(source, target):
+        copy = pltpu.make_async_copy(source, target, copy_sems.at[2 + len(results)])
+        copy.start()
+        results.append(copy)
 
     def swap(source, target, at, device, sems=swap_sems):
         copy = pltpu.make_async_remote_copy(
@@ -1102,6 +1210,7 @@
         to_row.append(
             begin(swap(hidden_part(x, at), hidden_row.at[:, there], per + at, across, piece_sems))
         )
+    result(up_grad, up_grad_out)
     second_x = begin(swap(second_theirs, second_came, 0, partner))
     gate_x = begin(swap(gate_grad, gate_came, 1, partner))
 
@@ -1137,41 +1246,6 @@
     pair_c = begin(swap(summed, col_came, 3, beside))
     gate_r = begin(swap(gate_grad, gate_row, 4, across))
     up_r = begin(swap(up_grad, up_row, 5, across))
-
-    def down_product(start, target, dtype):
-        def body(j, slot):
-            target[:, columns_at(j)] = mm(hidden[...], tall_tiles[slot, 0]).astype(dtype)
-
-        stream(
-            lambda j: [down_w.at[:, pl.ds(pl.multiple_of(start + j * 256, 256), 256)]],
-            lambda slot: [tall_tiles.at[slot, 0]],
-            tile_sems,
-            half // 256,
-            body,
-        )
-
-    pair_r.wait_send()
-    pending[:] = [copy for copy in pending if copy is not pair_r]
-    down_product(half, sent, BF16)
-    layer_r = begin(swap(sent, row_came.at[1], 7, across))
-    down_product(0, kept, F32)
-    layer_r.wait_recv()
-
-    def mine_of(value):
-        return jnp.where(col == 0, value[:, :block], value[:, block:])
-
-    def theirs_of(value):
-        return jnp.where(col == 0, value[:, block:], value[:, :block])
-
-    def join_layer(rows):
-        total = kept[rows, :] + row_came[1, rows, :].astype(F32)
-        layer_own[rows, :] = mine_of(total)
-        block_sent[0, rows, :] = theirs_of(total).astype(BF16)
-
-    rows_loop(join_layer)
-    layer_c = begin(swap(block_sent.at[0], block_came.at[0], 8, beside))
-    middle_in = pltpu.make_async_copy(middle, kept, copy_sems.at[0])
-    middle_in.start()
 
     for copy in to_x:
         copy.wait_recv()
@@ -1205,6 +1279,41 @@
     down_grad(1, lambda at: hidden_row.at[:, pl.ds(at * width, width)], hidden_came_row)
     down_line.run(0, 1)
 
+    def down_product(start, target, dtype):
+        def body(j, slot):
+            target[:, columns_at(j)] = mm(hidden[...], tall_tiles[slot, 0]).astype(dtype)
+
+        stream(
+            lambda j: [down_w.at[:, pl.ds(pl.multiple_of(start + j * 256, 256), 256)]],
+            lambda slot: [tall_tiles.at[slot, 0]],
+            tile_sems,
+            half // 256,
+            body,
+        )
+
+    pair_r.wait_send()
+    pending[:] = [copy for copy in pending if copy is not pair_r]
+    down_product(half, sent, BF16)
+    layer_r = begin(swap(sent, row_came.at[1], 7, across))
+    down_product(0, kept, F32)
+    layer_r.wait_recv()
+
+    def mine_of(value):
+        return jnp.where(col == 0, value[:, :block], value[:, block:])
+
+    def theirs_of(value):
+        return jnp.where(col == 0, value[:, block:], value[:, :block])
+
+    def join_layer(rows):
+        total = kept[rows, :] + row_came[1, rows, :].astype(F32)
+        layer_own[rows, :] = mine_of(total)
+        block_sent[0, rows, :] = theirs_of(total).astype(BF16)
+
+    rows_loop(join_layer)
+    layer_c = begin(swap(block_sent.at[0], block_came.at[0], 8, beside))
+    middle_in = pltpu.make_async_copy(middle, kept, copy_sems.at[0])
+    middle_in.start()
+
     middle_in.wait()
     pair_c.wait_recv()
     feed_sum[...] = jnp.zeros_like(feed_sum)
@@ -1237,8 +1346,11 @@
         layer_own[rows, :] += mine_of(held)
 
     rows_loop(norm_second_pass)
+    result(branch, branch_out)
     branch_r = begin(swap(branch, branch_row, 10, across))
     branch_r.wait_recv()
+
+    down_line.run(1, 2)
 
     def mixed_body(j, slot):
         total = mm_nt(branch[...], tiles[slot, :, :half])
@@ -1252,7 +1364,6 @@
         out_w.shape[0] // 256,
         mixed_body,
     )
-    down_line.run(1, 2)
     pairs = turned.shape[1] // 384
     lower = lax.broadcasted_iota(jnp.int32, (SL, SL), 1) <= lax.broadcasted_iota(
         jnp.int32, (SL, SL), 0
@@ -1282,6 +1393,7 @@
         return 0
 
     lax.fori_loop(0, MICRO * pairs, attend, 0)
+    result(dqkv, dqkv_out)
 
     def first_body(target, dtype):
         def body(j, slot):
@@ -1296,6 +1408,7 @@
     first_r = begin(swap(sent, row_came.at[2], 11, across))
     dqkv_r = begin(swap(dqkv, dqkv_row, 12, across))
     nt_product(qkv_w, dqkv.shape[1], 0, first_body(kept, F32))
+    down_line.run(2, line - 1)
     first_r.wait_recv()
 
     def join_first(rows):
@@ -1305,9 +1418,9 @@
 
     rows_loop(join_first)
     first_c = begin(swap(block_sent.at[1], block_came.at[1], 13, beside))
-    down_line.run(2, line - 1)
 
     second_x.wait_recv()
+    result(second_came, second_came_out)
     depth = second_mine.shape[0]
     turned_left[:, :depth] = second_mine[...].T
     turned_left[:, depth:] = second_came[...].T
@@ -1342,6 +1455,7 @@
         lambda j, slot: (tall_tiles[slot, 0, :ROWS], tall_tiles[slot, 1, :ROWS]),
     )
 
+    result(gate_grads, gate_grads_out)
     layer_c.wait_recv()
     first_c.wait_recv()
     attention_sum[...] = jnp.zeros_like(attention_sum)
@@ -1389,6 +1503,8 @@
     for copy in pending:
         copy.wait_send()
     down_store.wait()
+    for copy in results:
+        copy.wait()
 
 
 def chain(line, identity, *values):
@@ -1409,13 +1525,13 @@
 
     outs = [
         (array(2 * rows // line, half, dtype=F32), anywhere),
-        (array(narrow, 2 * quarter), vmem),
-        (array(ROWS, narrow), vmem),
-        (array(ROWS, quarter), vmem),
+        (array(narrow, 2 * quarter), anywhere),
+        (array(ROWS, narrow), anywhere),
         (array(ROWS, quarter), anywhere),
-        (array(ROWS, qkv_width), vmem),
+        (array(ROWS, quarter), anywhere),
         (array(ROWS, qkv_width), anywhere),
-        (array(ROWS, half), vmem),
+        (array(ROWS, qkv_width), anywhere),
+        (array(ROWS, half), anywhere),
         (array(2 * ROWS, block), vmem),
         (array(2, block, dtype=F32), vmem),
         (array(ROWS, quarter), anywhere),
@@ -1429,6 +1545,11 @@
         in_specs=[anywhere if k in outside else vmem for k in range(len(values))],
         out_specs=[place for _, place in outs],
         scratch_shapes=[
+            buffer(narrow, 2 * quarter),
+            buffer(ROWS, narrow),
+            buffer(ROWS, quarter),
+            buffer(ROWS, qkv_width),
+            buffer(ROWS, half),
             buffer(ROWS, quarter),
             buffer(ROWS, quarter),
             buffer(2, 256, 2 * quarter),
@@ -1459,7 +1580,7 @@
             sem((2, 3 * (line // 2))),
             sem((2, 3)),
             sem((2, 2, line - 1, 4)),
-            sem((2,)),
+            sem((7,)),
         ],
         compiler_params=pltpu.CompilerParams(
             collective_id=identity, has_side_effects=True, vmem_limit_bytes=67043328
@@ -1501,9 +1622,10 @@
             jax.ShapeDtypeStruct(both.shape, BF16),
             array(*gains.shape),
         ],
-        in_specs=[vmem] * 12 + [anywhere, vmem],
+        in_specs=[vmem] + [anywhere] * 12 + [vmem],
         out_specs=[anywhere] * 7 + [vmem],
-        scratch_shapes=[buffer(2, line - 1, *size) for size in sizes]
+        scratch_shapes=[buffer(*values[at].shape) for at in (1, 2, 3, 4, 5, 6, 7, 9, 10)]
+        + [buffer(2, line - 1, *size) for size in sizes]
         + [buffer(h, w) for h, w in zip(heights[1:], widths[1:])]
         + [buffer(*up.shape)] * 2
         + [buffer(*dqkv.shape)] * 2
@@ -1517,6 +1639,7 @@
         + [
             pltpu.SemaphoreType.DMA((2, both.shape[1])),
             pltpu.SemaphoreType.DMA((2, gain_steps)),
+            pltpu.SemaphoreType.DMA((9,)),
         ],
         compiler_params=pltpu.CompilerParams(
             collective_id=identity, has_side_effects=True, vmem_limit_bytes=67043328
@@ -1625,14 +1748,18 @@
         x_block,
         top_half,
         top_came,
-        normed_first,
+        first_mine,
+        first_theirs,
         turned,
-        mixed,
+        mixed_mine,
+        mixed_theirs,
         middle,
+        second_mine,
+        second_theirs,
+        normed_second,
+        hidden_grad,
         inverse_first,
         inverse_second,
-        normed_second,
-        hidden_grad,
         gains_half,
     ) = front(
         line,
@@ -1653,9 +1780,6 @@
     )
     x_block = x_block.reshape(ROWS, block)
     narrow = half // groups
-    first_mine, first_theirs = x_parts(normed_first[:, :half], narrow)
-    mixed_mine, mixed_theirs = x_parts(mixed, 2 * mixed.shape[1] // groups)
-    second_mine, second_theirs = x_parts(normed_second[:, :half], narrow)
     (
         down_sum,
         gate_grads,

time: 451 us -> 431 us (0.956)
  Pallas kernels: 441 us -> 426 us
    pallas_call x1, Pallas kernels: 234 us -> 228 us  [tail_sums(): pl.pallas_call(lambda *refs: tail_kernel(line, *refs), out_shape=[array(*...]
    pallas_call x1, Pallas kernels: 122 us -> 116 us  [chain(): pl.pallas_call(lambda *refs: chain_kernel(line, *refs), out_shape=[shape...]
where the time goes in v3:
time: 431 us; the launch traced here: 430 us
  Pallas kernels  426 us (99%)
    pallas_call x1, Pallas kernels, tail_sums(): pl.pallas_call(lambda *refs: tail_kernel(line, *refs), out_shape=[array(*...  228 us
    pallas_call x1, Pallas kernels, chain(): pl.pallas_call(lambda *refs: chain_kernel(line, *refs), out_shape=[shape...  116 us
    pallas_call x1, Pallas kernels, front(): pl.pallas_call(front_kernel, out_shape=[array(D, 2 * quarter), array(quar...  70.8 us

profile of v3, /device:TPU:0, one launch (start us, length us, event | category | flops | bytes accessed | tf_op | source)
XLA Modules:
  0.0 429.5 jit_solution(5504870911843201086)
XLA Ops:
  0.7 0.5 fusion
  1.2 1.1 pad_maximum_fusion.2
  2.3 2.4 shard_map.212
  4.7 70.8 %shard_map.213 = (bf16[2048,4096]{1,0:T(8,128)(2,1)}, bf16[2048,2048]{1,0:T(8,128)(2,1)}, bf16[2048,1536]{1,0:T(8,128)(2,1)}, bf16[512,2048]{1,0:T(8,128)(2,1)},...) custom-call(bf16[2,8,32,512]{3,2,1,0:T(8,128)(2,1)} %get-tuple-eleme, ...), custom_call_target="tpu_custom_call" | custom-call | tf_op jit(solution)/shard_map/pallas_call | solution.py:988
  75.5 116.4 %shard_map.214 = (f32[512,1024]{1,0:T(8,128)}, bf16[512,4096]{1,0:T(8,128)(2,1)}, bf16[512,512]{1,0:T(8,128)(2,1)}, bf16[512,2048]{1,0:T(8,128)(2,1)}, bf16[512,...) custom-call(bf16[512,2048]{1,0:T(8,128)(2,1)} %get-tuple-element.64., ...), custom_call_target="tpu_custom_call" | custom-call | tf_op jit(solution)/shard_map/pallas_call | solution.py:1542
  191.9 227.7 %shard_map.215 = (f32[128,4096]{1,0:T(8,128)}, f32[128,4096]{1,0:T(8,128)}, f32[128,1024]{1,0:T(8,128)}, f32[128,1024]{1,0:T(8,128)}, f32[128,1024]{1,0:T(8,128)...) custom-call(bf16[512,4096]{1,0:T(8,128)(2,1)} %get-tuple-element.80.refs_0_, ...), custom_call_target="tpu_custom_call" | custom-call | tf_op jit(solution)/shard_map/pallas_call | solution.py:1613
  419.7 8.6 %shard_map.216 = (bf16[2,8,32,512]{3,2,1,0:T(8,128)(2,1)}, bf16[2,8,32,512]{3,2,1,0:T(8,128)(2,1)}, f32[512,1024]{1,0:T(8,128)}, f32[128,4096]{1,0:T(8,128)}, f3...) custom-call(s32[2,8]{1,0:T(2,128)} %refs_0_.1, ...), custom_call_target="tpu_custom_call" | custom-call | tf_op jit(solution)/shard_map/pallas_call | solution.py:1681
  428.3 0.7 constant_dynamic-slice_fusion
  429.0 0.5 slice_bitcast_fusion
  (2 shorter events, 0.0 us)

commit v4 on v3

--- a/solution.py
+++ b/solution.py
@@ -2,6 +2,7 @@
 
 import jax
 import jax.numpy as jnp
+import numpy as np
 from jax import lax
 from jax.experimental import pallas as pl
 from jax.experimental.pallas import tpu as pltpu
@@ -36,17 +37,14 @@
 
 def rope_tables():
     half = HEAD_DIM // 2
-    frequency = jnp.exp(
-        jnp.arange(half, dtype=F32) * (-2.0 * math.log(ROPE_THETA) / HEAD_DIM)
-    )
-    angles = jnp.arange(SL, dtype=F32)[:, None] * frequency[None, :]
-    cosine = jnp.cos(angles)
-    sine = jnp.sin(angles)
-    zero = jnp.zeros_like(sine)
-    table_cos = jnp.concatenate([cosine] * 4, axis=1)
-    table_first = jnp.concatenate([sine, zero] * 2, axis=1)
-    table_second = jnp.concatenate([zero, sine] * 2, axis=1)
-    return table_cos, table_first, table_second
+    frequency = np.exp(np.arange(half, dtype=np.float32) * np.float32(-2.0 * math.log(ROPE_THETA) / HEAD_DIM))
+    angles = np.arange(SL, dtype=np.float32)[:, None] * frequency[None, :]
+    cosine, sine = np.cos(angles), np.sin(angles)
+    zero = np.zeros_like(sine)
+    table_cos = np.concatenate([cosine] * 4, axis=1)
+    table_first = np.concatenate([sine, zero] * 2, axis=1)
+    table_second = np.concatenate([zero, sine] * 2, axis=1)
+    return jnp.asarray(table_cos), jnp.asarray(table_first), jnp.asarray(table_second)
 
 
 def turn(v, cos, first, second):
@@ -67,10 +65,16 @@
 
 
 def softmax_of(q, k, allowed):
-    scores = mm_nt(q, k) * HEAD_DIM ** (-0.5)
-    scores = jnp.where(allowed, scores, MASKED_SCORE)
+    scores = jnp.where(allowed, mm_nt(q, k), MASKED_SCORE)
     exps = jnp.exp(scores - jnp.max(scores, axis=1, keepdims=True))
-    return exps / jnp.sum(exps, axis=1, keepdims=True)
+    return exps * (1.0 / jnp.sum(exps, axis=1, keepdims=True))
+
+
+def scaled_down(q):
+    return (q.astype(F32) * HEAD_DIM ** (-0.5)).astype(BF16)
+
+
+BLOCKS = ((slice(0, SL), SL),)
 
 
 FREE = pl.CostEstimate(flops=0, bytes_accessed=0, transcendentals=0)
@@ -84,36 +88,47 @@
     qr = turn(qkv[:, :128], cos, first, second).astype(BF16)
     kr = turn(qkv[:, 128:256], cos, first, second).astype(BF16)
     vr = qkv[:, 256:].astype(BF16)
-    out = jnp.zeros((SL, 128), F32)
+    zero = jnp.zeros_like(vr)
+    outs = [jnp.zeros((SL, 128), F32)]
+    scaled = scaled_down(qr)
     for head in range(2):
         mask = head_mask(head)
-        probs = softmax_of(jnp.where(mask, qr, jnp.zeros_like(qr)), kr, allowed).astype(BF16)
-        out = out + mm(probs, jnp.where(mask, vr, jnp.zeros_like(vr)))
-    return qr, kr, vr, out.astype(BF16)
+        q_own = jnp.where(mask, scaled, zero)
+        v_own = jnp.where(mask, vr, zero)
+        for at, (rows, keys) in enumerate(BLOCKS):
+            probs = softmax_of(q_own[rows], kr[:keys], allowed[rows, :keys]).astype(BF16)
+            outs[at] = outs[at] + mm(probs, v_own[:keys])
+    return qr, kr, vr, jnp.concatenate(outs, axis=0).astype(BF16)
 
 
 def head_grads(qr, kr, vr, od, allowed, cos, first, second):
-    dq = jnp.zeros((SL, 128), F32)
-    dk = jnp.zeros((SL, 128), F32)
-    dv = jnp.zeros((SL, 128), F32)
+    dq = [jnp.zeros((SL, 128), F32)]
+    dk = [jnp.zeros((SL, 128), F32)]
+    dv = [jnp.zeros((SL, 128), F32)]
     zero = jnp.zeros_like(qr)
+    scaled = scaled_down(qr)
     for head in range(2):
         mask = head_mask(head)
-        q_own = jnp.where(mask, qr, zero)
+        q_own = jnp.where(mask, scaled, zero)
         k_own = jnp.where(mask, kr, zero)
         od_own = jnp.where(mask, od, zero)
-        probs = softmax_of(q_own, kr, allowed)
-        d_probs = mm_nt(od_own, vr)
-        dv = dv + mm_tn(probs.astype(BF16), od_own)
-        inner = jnp.sum(probs * d_probs, axis=1, keepdims=True)
-        d_scores = (probs * (d_probs - inner)).astype(BF16)
-        dq = dq + mm(d_scores, k_own)
-        dk = dk + mm_tn(d_scores, q_own)
-    scale = HEAD_DIM ** (-0.5)
+        for at, (rows, keys) in enumerate(BLOCKS):
+            probs = softmax_of(q_own[rows], kr[:keys], allowed[rows, :keys])
+            d_probs = mm_nt(od_own[rows], vr[:keys])
+            dv[at] = dv[at] + mm_tn(probs.astype(BF16), od_own[rows])
+            inner = jnp.sum(probs * d_probs, axis=1, keepdims=True)
+            d_scores = (probs * (d_probs - inner)).astype(BF16)
+            dq[at] = dq[at] + mm(d_scores, k_own[:keys])
+            dk[at] = dk[at] + mm_tn(d_scores, q_own[rows])
+
+    def keys_sum(parts):
+        return parts[0]
+
+    dq = jnp.concatenate(dq, axis=0) * HEAD_DIM ** (-0.5)
     return (
-        turn_back(dq * scale, cos, first, second).astype(BF16),
-        turn_back(dk * scale, cos, first, second).astype(BF16),
-        dv.astype(BF16),
+        turn_back(dq, cos, first, second).astype(BF16),
+        turn_back(keys_sum(dk), cos, first, second).astype(BF16),
+        keys_sum(dv).astype(BF16),
     )
 
 

time: 431 us -> 429 us (level)
  no operation moved by 1% of the time
where the time goes in v4:
time: 429 us; the launch traced here: 428 us
  Pallas kernels  426 us (99%)
    pallas_call x1, Pallas kernels, tail_sums(): pl.pallas_call(lambda *refs: tail_kernel(line, *refs), out_shape=[array(*...  228 us
    pallas_call x1, Pallas kernels, chain(): pl.pallas_call(lambda *refs: chain_kernel(line, *refs), out_shape=[shape...  116 us
    pallas_call x1, Pallas kernels, front(): pl.pallas_call(front_kernel, out_shape=[array(D, 2 * quarter), array(quar...  70.8 us

profile of v4, /device:TPU:0, one launch (start us, length us, event | category | flops | bytes accessed | tf_op | source)
XLA Modules:
  0.0 427.9 jit_solution(13519053927287819618)
XLA Ops:
  0.6 2.5 shard_map.239
  3.1 70.8 %shard_map.240 = (bf16[2048,4096]{1,0:T(8,128)(2,1)}, bf16[2048,2048]{1,0:T(8,128)(2,1)}, bf16[2048,1536]{1,0:T(8,128)(2,1)}, bf16[512,2048]{1,0:T(8,128)(2,1)},...) custom-call(bf16[2,8,32,512]{3,2,1,0:T(8,128)(2,1)} %get-tuple-eleme, ...), custom_call_target="tpu_custom_call" | custom-call | tf_op jit(solution)/shard_map/pallas_call | solution.py:1003
  73.9 116.4 %shard_map.241 = (f32[512,1024]{1,0:T(8,128)}, bf16[512,4096]{1,0:T(8,128)(2,1)}, bf16[512,512]{1,0:T(8,128)(2,1)}, bf16[512,2048]{1,0:T(8,128)(2,1)}, bf16[512,...) custom-call(bf16[512,2048]{1,0:T(8,128)(2,1)} %get-tuple-element.64., ...), custom_call_target="tpu_custom_call" | custom-call | tf_op jit(solution)/shard_map/pallas_call | solution.py:1557
  190.3 227.7 %shard_map.242 = (f32[128,4096]{1,0:T(8,128)}, f32[128,4096]{1,0:T(8,128)}, f32[128,1024]{1,0:T(8,128)}, f32[128,1024]{1,0:T(8,128)}, f32[128,1024]{1,0:T(8,128)...) custom-call(bf16[512,4096]{1,0:T(8,128)(2,1)} %get-tuple-element.80.refs_0_, ...), custom_call_target="tpu_custom_call" | custom-call | tf_op jit(solution)/shard_map/pallas_call | solution.py:1628
  418.0 8.6 %shard_map.243 = (bf16[2,8,32,512]{3,2,1,0:T(8,128)(2,1)}, bf16[2,8,32,512]{3,2,1,0:T(8,128)(2,1)}, f32[512,1024]{1,0:T(8,128)}, f32[128,4096]{1,0:T(8,128)}, f3...) custom-call(s32[2,8]{1,0:T(2,128)} %refs_0_.1, ...), custom_call_target="tpu_custom_call" | custom-call | tf_op jit(solution)/shard_map/pallas_call | solution.py:1696
  426.6 0.7 constant_dynamic-slice_fusion
  427.3 0.5 slice_bitcast_fusion

commit v5 on v4

--- a/solution.py
+++ b/solution.py
@@ -1663,10 +1663,10 @@
     )(*values)
 
 
-def finish_kernel(count, order_ref, back_ref, *refs):
+def finish_kernel(count, order_ref, back_ref, gains_ref, *refs):
     sums, rest = refs[:count], refs[count:]
-    layer_ref, grad_ref = rest[:2]
-    outs, held, sems = rest[2 : 2 + count], rest[2 + count : 2 + 2 * count], rest[2 + 2 * count]
+    layer_ref, grad_ref, attention_ref, feed_ref = rest[:4]
+    outs, held, sems = rest[4 : 4 + count], rest[4 + count : 4 + 2 * count], rest[4 + 2 * count]
     groups = back_ref.shape[1]
     loads = [pltpu.make_async_copy(sums[k], held[k], sems.at[0, k]) for k in range(count)]
     stores = [pltpu.make_async_copy(held[k], outs[k], sems.at[1, k]) for k in range(count)]
@@ -1681,6 +1681,18 @@
         return 0
 
     lax.fori_loop(0, MICRO * groups, one, 0)
+    size = attention_ref.shape[1]
+    width = gains_ref.shape[1]
+    at = lax.broadcasted_iota(jnp.int32, (width, size), 0)
+    wanted = lax.broadcasted_iota(jnp.int32, (width, size), 1) + lax.axis_index("dp") * size
+    picked = jnp.dot(
+        gains_ref[...],
+        jnp.where(at == wanted, 1.0, 0.0),
+        preferred_element_type=F32,
+        precision=lax.Precision.HIGHEST,
+    )
+    attention_ref[...] = picked[0:1, :]
+    feed_ref[...] = picked[1:2, :]
     for load, store in zip(loads, stores):
         load.wait()
         store.start()
@@ -1688,20 +1700,21 @@
         store.wait()
 
 
-def finish(order, back, *sums):
+def finish(order, back, gains, *sums):
     vmem = pl.BlockSpec(memory_space=pltpu.VMEM)
     anywhere = pl.BlockSpec(memory_space=pl.ANY)
     rows = jax.ShapeDtypeStruct((MICRO,) + back.shape[1:], BF16)
+    part = jax.ShapeDtypeStruct((1, gains.shape[1] // back.shape[1]), F32)
     count = len(sums)
     return pl.pallas_call(
         lambda *refs: finish_kernel(count, *refs),
-        out_shape=[rows, rows] + [jax.ShapeDtypeStruct(v.shape, F32) for v in sums],
-        in_specs=[pl.BlockSpec(memory_space=pltpu.SMEM), vmem] + [anywhere] * count,
-        out_specs=[vmem, vmem] + [anywhere] * count,
+        out_shape=[rows, rows, part, part] + [jax.ShapeDtypeStruct(v.shape, F32) for v in sums],
+        in_specs=[pl.BlockSpec(memory_space=pltpu.SMEM), vmem, vmem] + [anywhere] * count,
+        out_specs=[vmem] * 4 + [anywhere] * count,
         scratch_shapes=[pltpu.VMEM(v.shape, F32) for v in sums]
         + [pltpu.SemaphoreType.DMA((2, count))],
         cost_estimate=FREE,
-    )(order, back, *sums)
+    )(order, back, gains, *sums)
 
 
 def per_device(
@@ -1858,6 +1871,8 @@
     (
         layer_output,
         tokens_grad,
+        attention_sum,
+        feed_sum,
         down_sum,
         gate_sum,
         up_sum,
@@ -1868,6 +1883,7 @@
     ) = finish(
         deal_order,
         back,
+        gain_sums,
         down_sum,
         gate_sum,
         up_sum,
@@ -1876,18 +1892,15 @@
         value_sum,
         output_sum,
     )
-    gain_size = block // groups
-    gain_sums = lax.dynamic_slice_in_dim(gain_sums, dp * gain_size, gain_size, 1)
-
     return (
         layer_output,
         tokens_grad,
-        gain_sums[0],
+        attention_sum.reshape(-1),
         query_sum,
         key_sum,
         value_sum,
         output_sum,
-        gain_sums[1],
+        feed_sum.reshape(-1),
         gate_sum,
         up_sum,
         down_sum,

time: 429 us -> 428 us (level)
  no operation moved by 1% of the time
where the time goes in v5:
time: 428 us; the launch traced here: 427 us
  Pallas kernels  426 us (100%)
    pallas_call x1, Pallas kernels, tail_sums(): pl.pallas_call(lambda *refs: tail_kernel(line, *refs), out_shape=[array(*...  228 us
    pallas_call x1, Pallas kernels, chain(): pl.pallas_call(lambda *refs: chain_kernel(line, *refs), out_shape=[shape...  116 us
    pallas_call x1, Pallas kernels, front(): pl.pallas_call(front_kernel, out_shape=[array(D, 2 * quarter), array(quar...  70.8 us
    pallas_call x1, Pallas kernels, finish(): pl.pallas_call(lambda *refs: finish_kernel(count, *refs), out_shape=[rows...  8.58 us

profile of v5, /device:TPU:0, one launch (start us, length us, event | category | flops | bytes accessed | tf_op | source)
XLA Modules:
  0.0 426.7 jit_solution(9554187413691010181)
XLA Ops:
  0.6 2.5 shard_map.239
  3.1 70.8 %shard_map.240 = (bf16[2048,4096]{1,0:T(8,128)(2,1)}, bf16[2048,2048]{1,0:T(8,128)(2,1)}, bf16[2048,1536]{1,0:T(8,128)(2,1)}, bf16[512,2048]{1,0:T(8,128)(2,1)},...) custom-call(bf16[2,8,32,512]{3,2,1,0:T(8,128)(2,1)} %get-tuple-eleme, ...), custom_call_target="tpu_custom_call" | custom-call | tf_op jit(solution)/shard_map/pallas_call | solution.py:1003
  73.9 116.4 %shard_map.241 = (f32[512,1024]{1,0:T(8,128)}, bf16[512,4096]{1,0:T(8,128)(2,1)}, bf16[512,512]{1,0:T(8,128)(2,1)}, bf16[512,2048]{1,0:T(8,128)(2,1)}, bf16[512,...) custom-call(bf16[512,2048]{1,0:T(8,128)(2,1)} %get-tuple-element.66., ...), custom_call_target="tpu_custom_call" | custom-call | tf_op jit(solution)/shard_map/pallas_call | solution.py:1557
  190.3 227.7 %shard_map.242 = (f32[128,4096]{1,0:T(8,128)}, f32[128,4096]{1,0:T(8,128)}, f32[128,1024]{1,0:T(8,128)}, f32[128,1024]{1,0:T(8,128)}, f32[128,1024]{1,0:T(8,128)...) custom-call(bf16[512,4096]{1,0:T(8,128)(2,1)} %get-tuple-element.82.refs_0_, ...), custom_call_target="tpu_custom_call" | custom-call | tf_op jit(solution)/shard_map/pallas_call | solution.py:1628
  417.9 8.6 %shard_map.243 = (bf16[2,8,32,512]{3,2,1,0:T(8,128)(2,1)}, bf16[2,8,32,512]{3,2,1,0:T(8,128)(2,1)}, f32[1,64]{1,0:T(1,128)}, f32[1,64]{1,0:T(1,128)}, f32[512,10...) custom-call(s32[2,8]{1,0:T(2,128)} %refs_0_.1, ...), custom_call_target="tpu_custom_call" | custom-call | tf_op jit(solution)/shard_map/pallas_call | solution.py:1709

commit v6 on v5

--- a/solution.py
+++ b/solution.py
@@ -431,7 +431,6 @@
         returned(step).start()
         return 0
 
-    lax.fori_loop(1, groups, send_back, 0)
     store(both.at[:, dp], back.at[:, dp])
 
     fetches[0].wait()
@@ -440,6 +439,7 @@
     turned_left[:, :depth] = second_mine[...].T
     turned_left[:, depth:] = second_came[...].T
     gate_line.run(1, 2)
+    lax.fori_loop(1, groups, send_back, 0)
 
     def wide(target, shift, mine, came):
         def body(columns, start):

time: 428 us -> 428 us (level)
  no operation moved by 1% of the time
where the time goes in v6:
time: 428 us; the launch traced here: 427 us
  Pallas kernels  426 us (100%)
    pallas_call x1, Pallas kernels, tail_sums(): pl.pallas_call(lambda *refs: tail_kernel(line, *refs), out_shape=[array(*...  228 us
    pallas_call x1, Pallas kernels, chain(): pl.pallas_call(lambda *refs: chain_kernel(line, *refs), out_shape=[shape...  116 us
    pallas_call x1, Pallas kernels, front(): pl.pallas_call(front_kernel, out_shape=[array(D, 2 * quarter), array(quar...  70.8 us
    pallas_call x1, Pallas kernels, finish(): pl.pallas_call(lambda *refs: finish_kernel(count, *refs), out_shape=[rows...  8.58 us

profile of v6, /device:TPU:0, one launch (start us, length us, event | category | flops | bytes accessed | tf_op | source)
XLA Modules:
  0.0 426.6 jit_solution(7525910424687159740)
XLA Ops:
  0.6 2.5 shard_map.239
  3.1 70.8 %shard_map.240 = (bf16[2048,4096]{1,0:T(8,128)(2,1)}, bf16[2048,2048]{1,0:T(8,128)(2,1)}, bf16[2048,1536]{1,0:T(8,128)(2,1)}, bf16[512,2048]{1,0:T(8,128)(2,1)},...) custom-call(bf16[2,8,32,512]{3,2,1,0:T(8,128)(2,1)} %get-tuple-eleme, ...), custom_call_target="tpu_custom_call" | custom-call | tf_op jit(solution)/shard_map/pallas_call | solution.py:1003
  73.9 116.4 %shard_map.241 = (f32[512,1024]{1,0:T(8,128)}, bf16[512,4096]{1,0:T(8,128)(2,1)}, bf16[512,512]{1,0:T(8,128)(2,1)}, bf16[512,2048]{1,0:T(8,128)(2,1)}, bf16[512,...) custom-call(bf16[512,2048]{1,0:T(8,128)(2,1)} %get-tuple-element.66., ...), custom_call_target="tpu_custom_call" | custom-call | tf_op jit(solution)/shard_map/pallas_call | solution.py:1557
  190.3 227.5 %shard_map.242 = (f32[128,4096]{1,0:T(8,128)}, f32[128,4096]{1,0:T(8,128)}, f32[128,1024]{1,0:T(8,128)}, f32[128,1024]{1,0:T(8,128)}, f32[128,1024]{1,0:T(8,128)...) custom-call(bf16[512,4096]{1,0:T(8,128)(2,1)} %get-tuple-element.82.refs_0_, ...), custom_call_target="tpu_custom_call" | custom-call | tf_op jit(solution)/shard_map/pallas_call | solution.py:1628
  417.8 8.6 %shard_map.243 = (bf16[2,8,32,512]{3,2,1,0:T(8,128)(2,1)}, bf16[2,8,32,512]{3,2,1,0:T(8,128)(2,1)}, f32[1,64]{1,0:T(1,128)}, f32[1,64]{1,0:T(1,128)}, f32[512,10...) custom-call(s32[2,8]{1,0:T(2,128)} %refs_0_.1, ...), custom_call_target="tpu_custom_call" | custom-call | tf_op jit(solution)/shard_map/pallas_call | solution.py:1709
